TPU v7x, 32 devices: a whole 2x2x4 slice. The times are simulated.
32 devices in a mesh: ta: 4 (over y, x), gx: 2 (over core), gy: 4 (over z).
Axes of the slice: x: 2, y: 2, z: 4, core: 2. Of those that a mesh axis runs over, the one named last changes fastest.
Arguments:
- feat: bfloat16 [4, 2, 4, 768, 128], P('ta', 'gx', 'gy'), may hold values from -6 to 6
- ref_feat: bfloat16 [4, 2, 4, 768, 128], P('ta', 'gx', 'gy'), may hold values from -6 to 6
- rim_rows: int32 [4, 2, 4, 48], P('ta', 'gx', 'gy'), may hold values from 0 to 767
- nbr: int32 [4, 2, 4, 27, 768], P('ta', 'gx', 'gy'), may hold values from 0 to 1200, as said below
- send_blocks: int32 [4, 2, 4, 8, 2], P('ta', 'gx', 'gy'), may hold values from 0 to 5
- send_count: int32 [4, 2, 4, 8], P('ta', 'gx', 'gy'), may hold values from 0 to 2, as said below
- match_slot: int32 [4, 2, 4, 6], P('ta', 'gx', 'gy'), may hold values from 0 to 16, as said below
- labels: int32 [4, 2, 4, 768], P('ta', 'gx', 'gy'), may hold values 0 or 1
- conv_weight: bfloat16 [27, 128, 128], replicated, may hold values from -0.109375 to 0.109375
- ref_weight: bfloat16 [128, 128], replicated, may hold values from -0.5 to 0.5
- cls_weight: bfloat16 [128], replicated, may hold values from -1.796875 to 1.796875
Outputs:
- features_out: bfloat16 [4, 2, 4, 768, 128], P('ta', 'gx', 'gy')
- feature_grad: bfloat16 [4, 2, 4, 768, 128], P('ta', 'gx', 'gy')
- weight_grad: float32 [27, 128, 128], replicated
- ref_grad: float32 [128, 128], replicated
Inputs may be any that keep to these rules, and one draw needn't show every extreme that they name: `nbr`: rows index the brick's 768 rows, then the 432 rim rows of the 3 x 3 bricks around it (x outer, own brick in the middle), then the zero row; offset 13 of a voxel is the voxel itself. `send_count`: every brick sends 2 blocks to its own brick, and in each frame one brick drawn from the seed receives 2 blocks from every brick. `match_slot`: 16 means no match; every brick has one or more unmatched blocks.
All inputs are finite; a program needn't handle non-finite values. No bound on the sum of `labels` on one device may be relied on, other than what follows from the above.
Results may differ from a plain program's by a relative error of at most 0.0053.
Values may be sent and summed in bfloat16 or wider, within the bound.
A program may use at most 64 MiB of HBM per device.

v0:
```python
import math

import jax
import jax.numpy as jnp
from jax import lax
from jax.sharding import PartitionSpec as P

BLOCK = 128


loss_scale = 16.0


def with_halo(block, sides, width):
    for axis, dim in sides:
        count = lax.axis_size(axis)
        forward = [(i, i + 1) for i in range(count - 1)]
        backward = [(target, source) for source, target in forward]
        low = lax.ppermute(
            lax.slice_in_dim(block, block.shape[dim] - width, None, axis=dim), axis, forward
        )
        high = lax.ppermute(lax.slice_in_dim(block, 0, width, axis=dim), axis, backward)
        block = jnp.concatenate([low, block, high], axis=dim)
    return block


def passed_along(block, axis, distance):
    devices = range(lax.axis_size(axis))
    route = [(i - distance, i) for i in devices if i - distance in devices]
    return lax.ppermute(block, axis, route)


def pack_blocks(source, lists, counts):
    channels = source.shape[1]
    blocks = source.reshape(-1, BLOCK, channels)
    picked = blocks[lists]
    keep = jnp.arange(lists.shape[1])[None, :] < counts[:, None]
    return jnp.where(keep[:, :, None, None], picked, jnp.zeros_like(picked))


def route_blocks(buffer):
    result = lax.all_to_all(buffer, ("gx", "gy"), split_axis=0, concat_axis=0, tiled=True)
    return result


def selector(index_block, width):
    return (index_block[:, None] == jnp.arange(width, dtype=jnp.int32)[None, :]).astype(
        jnp.bfloat16
    )


def per_device(
    feat,
    ref_feat,
    rim_rows,
    nbr,
    send_blocks,
    send_count,
    match_slot,
    labels,
    conv_weight,
    ref_weight,
    cls_weight,
):
    current = feat[0, 0, 0]
    rows_here = current.shape[0]
    channels = current.shape[1]
    rim_index = rim_rows[0, 0, 0]
    rim_count = rim_index.shape[0]
    rim_feat = current[rim_index]
    padded = with_halo(rim_feat[None, None, None], (("gx", 1), ("gy", 2)), 1)
    halo_rows = padded[0].reshape(9 * rim_count, channels)
    extended = jnp.concatenate([current, halo_rows, jnp.zeros((1, channels), jnp.bfloat16)], axis=0)
    ext_rows = extended.shape[0]
    routed = route_blocks(pack_blocks(ref_feat[0, 0, 0], send_blocks[0, 0, 0], send_count[0, 0, 0]))
    received = passed_along(routed, "ta", 1)
    table = jnp.concatenate(
        [received.reshape(-1, BLOCK, channels), jnp.zeros((1, BLOCK, channels), jnp.bfloat16)],
        axis=0,
    )
    matched = table[match_slot[0, 0, 0]].reshape(rows_here, channels)
    offsets_map = nbr[0, 0, 0]
    row_block = math.gcd(256, rows_here)
    block_count = rows_here // row_block

    def gather_offset(index_row):

        def one_block(index_block):
            return jnp.dot(
                selector(index_block, ext_rows), extended, preferred_element_type=jnp.float32
            ).astype(jnp.bfloat16)

        return lax.map(one_block, index_row.reshape(block_count, row_block)).reshape(
            rows_here, channels
        )

    def forward_step(total, pair):
        index_row, weight = pair
        return (
            total + jnp.dot(gather_offset(index_row), weight, preferred_element_type=jnp.float32),
            None,
        )

    conv_sum = lax.scan(
        forward_step, jnp.zeros((rows_here, channels), jnp.float32), (offsets_map, conv_weight)
    )[0]
    preact = conv_sum + jnp.dot(matched, ref_weight, preferred_element_type=jnp.float32)
    activ = jax.nn.silu(preact).astype(jnp.bfloat16)
    logits = jnp.dot(activ, cls_weight, preferred_element_type=jnp.float32)
    resid = jax.nn.sigmoid(logits) - labels[0, 0, 0].astype(jnp.float32)
    sigmas = jax.nn.sigmoid(preact)
    pre_grad = (
        loss_scale
        * resid[:, None]
        * cls_weight.astype(jnp.float32)[None, :]
        * sigmas
        * (1.0 + preact * (1.0 - sigmas))
    ).astype(jnp.bfloat16)
    grad_blocks = pre_grad.reshape(block_count, row_block, channels)
    ext_wide = extended.astype(jnp.float32)

    def backward_step(grads, pair):
        index_row, weight = pair

        def add_block(collected, inputs):
            index_block, grad_block = inputs
            spread = lax.dot_general(
                selector(index_block, ext_rows),
                grad_block,
                (((0,), (0,)), ((), ())),
                preferred_element_type=jnp.float32,
            )
            return (collected + spread, None)

        collected = lax.scan(
            add_block,
            jnp.zeros((ext_rows, channels), jnp.float32),
            (index_row.reshape(block_count, row_block), grad_blocks),
        )[0]
        input_term = lax.dot_general(
            collected,
            weight.astype(jnp.float32),
            (((1,), (1,)), ((), ())),
            precision=lax.Precision.HIGHEST,
            preferred_element_type=jnp.float32,
        )
        weight_term = lax.dot_general(
            ext_wide,
            collected,
            (((0,), (0,)), ((), ())),
            precision=lax.Precision.HIGHEST,
            preferred_element_type=jnp.float32,
        )
        return (grads + input_term, weight_term)

    ext_grad, weight_terms = lax.scan(
        backward_step, jnp.zeros((ext_rows, channels), jnp.float32), (offsets_map, conv_weight)
    )
    ref_term = lax.dot_general(
        matched, pre_grad, (((0,), (0,)), ((), ())), preferred_element_type=jnp.float32
    )
    weight_grad, ref_grad = lax.psum((weight_terms, ref_term), ("ta", "gx", "gy"))
    halo_grad = ext_grad[rows_here : rows_here + 9 * rim_count].reshape(3, 3, rim_count, channels)
    column = halo_grad[1]
    for slot_x in (0, 2):
        column = column + passed_along(
            halo_grad[slot_x].astype(jnp.bfloat16), "gx", slot_x - 1
        ).astype(jnp.float32)
    rim_grad = column[1]
    for slot_y in (0, 2):
        rim_grad = rim_grad + passed_along(column[slot_y], "gy", slot_y - 1)
    feature_grad = ext_grad[:rows_here].at[rim_index].add(rim_grad).astype(jnp.bfloat16)
    return (activ[None, None, None], feature_grad[None, None, None], weight_grad, ref_grad)


def solution(mesh):
    placed = (
        P("ta", "gx", "gy", None, None),
        P("ta", "gx", "gy", None, None),
        P("ta", "gx", "gy", None),
        P("ta", "gx", "gy", None, None),
        P("ta", "gx", "gy", None, None),
        P("ta", "gx", "gy", None),
        P("ta", "gx", "gy", None),
        P("ta", "gx", "gy", None),
        P(),
        P(),
        P(),
    )
    return jax.shard_map(
        per_device,
        mesh=mesh,
        in_specs=placed,
        out_specs=(P("ta", "gx", "gy", None, None), P("ta", "gx", "gy", None, None), P(), P()),
        check_vma=False,
    )
```

profile of v0, /device:TPU:0, one launch (start us, length us, event | category | flops | bytes accessed | tf_op | source)
XLA Modules:
  0.0 417.6 jit_solution(17842719971081728127)
XLA Ops:
  10.8 3.0 collective-permute-start
  17.0 6.4 %all-to-all-start = ((bf16[8,2,128,128]{3,2,1,0:T(8,128)(2,1)}), bf16[8,2,128,128]{3,2,1,0:T(8,128)(2,1)S(1)}, u32[]{:S(2)}, u32[]{:S(2)}) async-start(bf16[8,2,128,128]{3,2,1,0:T(8,128)(2,1)} %broadcast_select_fusion), calls=%async_computation | async-start | bytes 1048576 | tf_op jit(solution)/shard_map/all_to_all | solution.py:42
  24.8 4.5 %collective-permute-start.2 = (bf16[1,3,1,48,128]{4,3,2,1,0:T(8,128)(2,1)S(1)}, bf16[1,3,1,48,128]{4,3,2,1,0:T(8,128)(2,1)S(1)}, u32[]{:S(2)}, u32[]{:S(2)}) collective-permute-start(bf16[1,3,1,48,128]{4,3,2,1,0:T(8,128)(2,1)S(1)} %pad_maximum_fusion.1), channel_id=1, source_target_pairs={{0,1},{1,2},{2,3},{4,5},{5,6},{6,7},{8,9},{9,10},{10,11},{12,13},{... | collective-permute-start | bytes 110600 | tf_op jit(solution)/shard_map/ppermute | solution.py:19
  30.6 3.2 collective-permute-done.2
  34.1 4.1 all-to-all-done
  38.1 3.4 collective-permute-start.4
  41.6 66.2 %while.48 = (s32[]{:T(128)}, f32[768,128]{1,0:T(8,128)S(1)}, s32[27,768]{1,0:T(8,128)S(1)}, bf16[1201,128]{1,0:T(8,128)(2,1)S(1)}, bf16[27,128,128]{2,1,0:T(8,128)(2,1)}, /*index=5*/s32[]{:T(128)}, s32[]{:T(128)}, s32[]{:T(128)}) while((s32[]{:T(128)}, f32[768,128]{1,0:T(8,128)S(1)}, s32[27,768]{1,0:T(8,128)S(1)}, ...), condition=%wide.region_3.4_spmd.clone, body=%wide.region_0.3_spmd.clone.sunk | while | flops 104411392 | bytes 1406188 | solution.py:104
  110.7 163.7 %while.50 = (s32[]{:T(128)}, f32[1201,128]{1,0:T(8,128)S(1)}, f32[27,128,128]{2,1,0:T(8,128)}, s32[27,768]{1,0:T(8,128)S(1)}, bf16[3,256,128]{2,1,0:T(8,128)(2,1...) while((s32[]{:T(128)}, f32[1201,128]{1,0:T(8,128)S(1)}, ...), condition=%wide.region_7.8_spmd.clone, body=%wide.region_4.7_spmd.clone.sunk | while | flops 551883520 | bytes 4749602 | solution.py:156
  110.8 2.4 while.52
  114.4 1.7 convolution_add_fusion.8
  116.9 2.4 while.52
  120.5 1.7 convolution_add_fusion.8
  122.9 2.4 while.52
  126.5 1.7 convolution_add_fusion.8
  129.0 2.4 while.52
  132.6 1.7 convolution_add_fusion.8
  135.0 2.4 while.52
  138.6 1.7 convolution_add_fusion.8
  141.1 2.4 while.52
  144.7 1.7 convolution_add_fusion.8
  147.2 2.4 while.52
  150.8 1.7 convolution_add_fusion.8
  153.2 2.4 while.52
  156.8 1.7 convolution_add_fusion.8
  159.3 2.4 while.52
  162.9 1.7 convolution_add_fusion.8
  165.4 2.4 while.52
  169.0 1.7 convolution_add_fusion.8
  171.4 2.4 while.52
  175.0 1.7 convolution_add_fusion.8
  177.5 2.4 while.52
  181.1 1.7 convolution_add_fusion.8
  183.5 2.4 while.52
  187.2 1.7 convolution_add_fusion.8
  189.6 2.4 while.52
  193.2 1.7 convolution_add_fusion.8
  195.7 2.4 while.52
  199.3 1.7 convolution_add_fusion.8
  201.7 2.4 while.52
  205.3 1.7 convolution_add_fusion.8
  207.8 2.4 while.52
  211.4 1.7 convolution_add_fusion.8
  213.9 2.4 while.52
  217.5 1.7 convolution_add_fusion.8
  219.9 2.4 while.52
  223.5 1.7 convolution_add_fusion.8
  226.0 2.4 while.52
  229.6 1.7 convolution_add_fusion.8
  232.1 2.4 while.52
  235.7 1.7 convolution_add_fusion.8
  238.1 2.4 while.52
  241.7 1.7 convolution_add_fusion.8
  244.2 2.4 while.52
  250.2 2.4 while.52
  256.3 2.4 while.52
  259.9 1.7 convolution_add_fusion.8
  262.4 2.4 while.52
  266.0 1.7 convolution_add_fusion.8
  268.4 2.4 while.52
  274.5 2.4 collective-permute-start.6
  278.3 1.8 collective-permute-done.5
  281.4 4.5 %collective-permute-start.8 = (f32[48,128]{1,0:T(8,128)S(1)}, f32[48,128]{1,0:T(8,128)S(1)}, u32[]{:S(2)}, u32[]{:S(2)}) collective-permute-start(f32[48,128]{1,0:T(8,128)S(1)} %get-tuple-element.227), channel_id=1, source_target_pairs={{0,1},{1,2},{2,3},{4,5},{5,6},{6,7},{8,9},{9,10},{10,11},{12,13},{... | collective-permute-start | bytes 73736 | tf_op jit(solution)/shard_map/ppermute | solution.py:30
  289.2 118.0 %all-reduce.4.cloned.1.call-done = (f32[27,128,128]{2,1,0:T(8,128)}, f32[128,128]{1,0:T(8,128)}) async-done(((f32[27,128,128]{2,1,0:T(8,128)}, f32[128,128]{1,0:T(8,128)}), (f32[27,128,128]{2,1,0:T(8,128)}, f32[128,128]{1,0:T(8,128)})) %all-reduce.4.cloned.1.call-update) | async-done | bytes 1835024 | tf_op jit(solution)/shard_map/psum | solution.py:162
  407.2 2.9 copy.60
  (691 shorter events, 238.4 us)
Async XLA Ops:
  7.2 8.3 %copy-start = (bf16[1,1,1,768,128]{4,3,2,1,0:T(8,128)(2,1)S(1)}, bf16[1,1,1,768,128]{4,3,2,1,0:T(8,128)(2,1)}, u32[]{:S(2)}) copy-start(bf16[1,1,1,768,128]{4,3,2,1,0:T(8,128)(2,1)} %param.20) | copy-start | bytes 589828
  7.2 16.3 %copy-start.7 = (s32[1,1,1,6]{3,2,1,0:T(1,128)S(1)}, s32[1,1,1,6]{3,2,1,0:T(1,128)}, u32[]{:S(2)}) copy-start(s32[1,1,1,6]{3,2,1,0:T(1,128)} %param.25) | copy-start | bytes 76
  7.2 16.3 %copy-start.5 = (s32[1,1,1,768]{3,2,1,0:T(1,128)S(1)}, s32[1,1,1,768]{3,2,1,0:T(1,128)}, u32[]{:S(2)}) copy-start(s32[1,1,1,768]{3,2,1,0:T(1,128)} %param.26) | copy-start | bytes 9220
  7.2 22.2 %copy-start.6 = (bf16[128]{0:T(256)(128)(2,1)S(1)}, bf16[128]{0:T(256)(128)(2,1)}, u32[]{:S(2)}) copy-start(bf16[128]{0:T(256)(128)(2,1)} %param.29) | copy-start | bytes 772
  7.2 22.2 %copy-start.3 = (s32[1,1,1,27,768]{4,2,3,1,0:T(1,128)S(1)}, s32[1,1,1,27,768]{4,2,3,1,0:T(1,128)}, u32[]{:S(2)}) copy-start(s32[1,1,1,27,768]{4,2,3,1,0:T(1,128)} %param.22) | copy-start | bytes 248836
  9.5 13.9 %collective-permute-start.1 = (bf16[1,1,1,48,128]{4,3,2,1,0:T(8,128)(2,1)S(1)}, bf16[1,1,1,48,128]{4,3,2,1,0:T(8,128)(2,1)S(1)}, u32[]{:S(2)}, u32[]{:S(2)}) collective-permute-start(bf16[1,1,1,48,128]{4,3,2,1,0:T(8,128)(2,1)S(1)} %bitcast.116), channel_id=1, source_target_pairs={{4,0},{5,1},{6,2},{7,3},{12,8},{13,9},{14,10},{15,11},{20,16},{21,... | collective-permute-start | bytes 36872 | tf_op jit(solution)/shard_map/ppermute | solution.py:22
  10.8 12.7 %collective-permute-start = (bf16[1,1,1,48,128]{4,3,2,1,0:T(8,128)(2,1)S(1)}, bf16[1,1,1,48,128]{4,3,2,1,0:T(8,128)(2,1)S(1)}, u32[]{:S(2)}, u32[]{:S(2)}) collective-permute-start(bf16[1,1,1,48,128]{4,3,2,1,0:T(8,128)(2,1)S(1)} %bitcast.117), channel_id=1, source_target_pairs={{0,4},{1,5},{2,6},{3,7},{8,12},{9,13},{10,14},{11,15},{16,20},{17,... | collective-permute-start | bytes 36872 | tf_op jit(solution)/shard_map/ppermute | solution.py:19
  15.5 18.4 %copy-start.1 = (bf16[1,1,1,768,128]{4,3,2,1,0:T(8,128)(2,1)S(1)}, bf16[1,1,1,768,128]{4,3,2,1,0:T(8,128)(2,1)}, u32[]{:S(2)}) copy-start(bf16[1,1,1,768,128]{4,3,2,1,0:T(8,128)(2,1)} %param.19) | copy-start | bytes 589828
  17.0 21.1 %all-to-all-start = ((bf16[8,2,128,128]{3,2,1,0:T(8,128)(2,1)}), bf16[8,2,128,128]{3,2,1,0:T(8,128)(2,1)S(1)}, u32[]{:S(2)}, u32[]{:S(2)}) async-start(bf16[8,2,128,128]{3,2,1,0:T(8,128)(2,1)} %broadcast_select_fusion), calls=%async_computation | async-start | bytes 1048576 | tf_op jit(solution)/shard_map/all_to_all | solution.py:42
  23.4 383.8 %all-reduce.4.cloned.1.call-start = ((), (), s32[]{:S(2)}) async-start(), calls=%async_computation.1 | async-start | bytes 3670016 | tf_op jit(solution)/shard_map/psum | solution.py:162
  23.5 7.1 %collective-permute-start.3 = (bf16[1,3,1,48,128]{4,3,2,1,0:T(8,128)(2,1)S(1)}, bf16[1,3,1,48,128]{4,3,2,1,0:T(8,128)(2,1)S(1)}, u32[]{:S(2)}, u32[]{:S(2)}) collective-permute-start(bf16[1,3,1,48,128]{4,3,2,1,0:T(8,128)(2,1)S(1)} %pad_maximum_fusion.1), channel_id=1, source_target_pairs={{1,0},{2,1},{3,2},{5,4},{6,5},{7,6},{9,8},{10,9},{11,10},{13,12},{... | collective-permute-start | bytes 110600 | tf_op jit(solution)/shard_map/ppermute | solution.py:22
  24.8 9.0 %collective-permute-start.2 = (bf16[1,3,1,48,128]{4,3,2,1,0:T(8,128)(2,1)S(1)}, bf16[1,3,1,48,128]{4,3,2,1,0:T(8,128)(2,1)S(1)}, u32[]{:S(2)}, u32[]{:S(2)}) collective-permute-start(bf16[1,3,1,48,128]{4,3,2,1,0:T(8,128)(2,1)S(1)} %pad_maximum_fusion.1), channel_id=1, source_target_pairs={{0,1},{1,2},{2,3},{4,5},{5,6},{6,7},{8,9},{9,10},{10,11},{12,13},{... | collective-permute-start | bytes 110600 | tf_op jit(solution)/shard_map/ppermute | solution.py:19
  38.1 69.6 %collective-permute-start.4 = (bf16[8,2,128,128]{3,2,1,0:T(8,128)(2,1)S(1)}, bf16[8,2,128,128]{3,2,1,0:T(8,128)(2,1)S(1)}, u32[]{:S(2)}, u32[]{:S(2)}) collective-permute-start(bf16[8,2,128,128]{3,2,1,0:T(8,128)(2,1)S(1)} %all-to-all-done), channel_id=1, source_target_pairs={{0,8},{8,16},{16,24},{1,9},{9,17},{17,25},{2,10},{10,18},{18,26},{... | collective-permute-start | bytes 1572872 | tf_op jit(solution)/shard_map/ppermute | solution.py:30
  109.4 1.3 copy-start.2
  274.5 3.7 collective-permute-start.6
  277.0 3.1 collective-permute-start.5
  280.1 5.9 %collective-permute-start.7 = (f32[48,128]{1,0:T(8,128)S(1)}, f32[48,128]{1,0:T(8,128)S(1)}, u32[]{:S(2)}, u32[]{:S(2)}) collective-permute-start(f32[48,128]{1,0:T(8,128)S(1)} %get-tuple-element.226), channel_id=1, source_target_pairs={{1,0},{2,1},{3,2},{5,4},{6,5},{7,6},{9,8},{10,9},{11,10},{13,12},{... | collective-permute-start | bytes 73736 | tf_op jit(solution)/shard_map/ppermute | solution.py:30
  281.4 6.1 %collective-permute-start.8 = (f32[48,128]{1,0:T(8,128)S(1)}, f32[48,128]{1,0:T(8,128)S(1)}, u32[]{:S(2)}, u32[]{:S(2)}) collective-permute-start(f32[48,128]{1,0:T(8,128)S(1)} %get-tuple-element.227), channel_id=1, source_target_pairs={{0,1},{1,2},{2,3},{4,5},{5,6},{6,7},{8,9},{9,10},{10,11},{12,13},{... | collective-permute-start | bytes 73736 | tf_op jit(solution)/shard_map/ppermute | solution.py:30
  407.2 2.9 copy-start.4
Sparse Core Ops, SparseCore 0:
  274.6 132.5 all-reduce.3
where the time goes:
time: 422 us; the launch traced here: 418 us
  matrix products  202 us (48%)
  waiting for transfers between devices  130 us (31%)
  starting transfers between devices  29.5 us (7%)
  local copies, waits for them, and re-layouts  29.1 us (7%)
  between operations  14.4 us (3%)
  loops' own time  7.23 us (2%)
  other arithmetic  5.42 us (1%)
    psum x1, waiting for transfers between devices, per_device(): lax.psum((weight_terms, ref_term), ('ta', 'gx', 'gy'))  118 us
    dot_general x81, matrix products, add_block(): lax.dot_general(selector(index_block, ext_rows), grad_block, (((0,), (0,)...  60.4 us
    dot_general x27, matrix products, backward_step(): lax.dot_general(collected, weight.astype(jnp.float32), (((1,), (1,)), (()...  45.2 us
    dot_general x81, matrix products, one_block(): jnp.dot(selector(index_block, ext_rows), extended, preferred_element_type...  34.2 us
    dot_general x27, matrix products, backward_step(): lax.dot_general(ext_wide, collected, (((0,), (0,)), ((), ())), precision=...  33.3 us
    dot_general x27, matrix products, forward_step(): jnp.dot(gather_offset(index_row), weight, preferred_element_type=jnp.floa...  27.1 us
    dynamic_update_slice x54, local copies, waits for them, and re-layouts, per_device(): lax.scan(backward_step, jnp.zeros((ext_rows, channels), jnp.float32), (of...  19.7 us
    ppermute x5, starting transfers between devices, passed_along(): return lax.ppermute(block, axis, route)  13 us
  transfers between devices with their start and end apart: 11, of which 6 were waited for; matrix products, arithmetic and copies ran while one was open for 16% of the time, Pallas kernels for 0%

commit v1 on v0

v1 whole, which is shorter than its diff:
```python
import functools

import jax
import jax.numpy as jnp
from jax import lax
from jax.experimental import pallas as pl
from jax.experimental.pallas import tpu as pltpu
from jax.sharding import PartitionSpec as P

BLOCK = 128
GROUP = 256
MESH = pl.DeviceIdType.MESH

loss_scale = 16.0


def with_halo(block, sides, width):
    for axis, dim in sides:
        count = lax.axis_size(axis)
        forward = [(i, i + 1) for i in range(count - 1)]
        backward = [(target, source) for source, target in forward]
        low = lax.ppermute(
            lax.slice_in_dim(block, block.shape[dim] - width, None, axis=dim), axis, forward
        )
        high = lax.ppermute(lax.slice_in_dim(block, 0, width, axis=dim), axis, backward)
        block = jnp.concatenate([low, block, high], axis=dim)
    return block


def passed_along(block, axis, distance):
    devices = range(lax.axis_size(axis))
    route = [(i - distance, i) for i in devices if i - distance in devices]
    return lax.ppermute(block, axis, route)


def pack_blocks(source, lists, counts):
    channels = source.shape[1]
    blocks = source.reshape(-1, BLOCK, channels)
    picked = blocks[lists]
    keep = jnp.arange(lists.shape[1])[None, :] < counts[:, None]
    return jnp.where(keep[:, :, None, None], picked, jnp.zeros_like(picked))


def route_blocks(buffer):
    return lax.all_to_all(buffer, ("gx", "gy"), split_axis=0, concat_axis=0, tiled=True)


def brick_kernel(
    offsets, groups, ext_ref, matched_ref, nbr_ref, labels_ref, weight_ref, cls_ref,
    activ_ref, own_ref, halo_ref, terms_ref,
    table, onehot, gathered, acc, pgrad,
):
    rows, channels = activ_ref.shape
    center = offsets // 2
    table[...] = jnp.zeros_like(table)
    ext_rows = ext_ref.shape[0]
    for g in range(groups):
        width = min(GROUP, ext_rows - g * GROUP)
        table[pl.ds(g * channels, channels), pl.ds(0, width)] = (
            ext_ref[pl.ds(g * GROUP, width), :].T
        )
    gathered[pl.ds(center * channels, channels), :] = ext_ref[pl.ds(0, rows), :].T
    gathered[pl.ds(offsets * channels, channels), :] = matched_ref[...].T
    slot = lax.broadcasted_iota(jnp.int32, (GROUP, rows), 0)

    def gather_step(j, total):
        o = j + (j >= center).astype(jnp.int32)
        index = nbr_ref[o]
        hit = (slot == (index & (GROUP - 1))).astype(jnp.float32).astype(jnp.bfloat16)
        onehot[o] = hit
        wide = jnp.dot(table[...], hit, preferred_element_type=jnp.float32)
        part = index // GROUP
        picked = wide[:channels]
        for g in range(1, groups):
            picked = jnp.where(part == g, wide[g * channels : (g + 1) * channels], picked)
        picked = picked.astype(jnp.bfloat16)
        gathered[pl.ds(pl.multiple_of(o * channels, channels), channels), :] = picked
        return total + jnp.dot(weight_ref[o].T, picked, preferred_element_type=jnp.float32)

    preact = jnp.zeros((channels, rows), jnp.float32)
    for o in (center, offsets):
        preact += jnp.dot(
            weight_ref[o].T,
            gathered[pl.ds(o * channels, channels), :],
            preferred_element_type=jnp.float32,
        )
    preact = lax.fori_loop(0, offsets - 1, gather_step, preact)
    sigmas = jax.nn.sigmoid(preact)
    activ = (preact * sigmas).astype(jnp.bfloat16)
    activ_ref[...] = activ.T
    scale = cls_ref[...].astype(jnp.float32)
    logits = jnp.sum(activ.astype(jnp.float32) * scale, axis=0, keepdims=True)
    resid = jax.nn.sigmoid(logits) - labels_ref[...].astype(jnp.float32)
    pgrad[...] = (
        loss_scale * resid * scale * sigmas * (1.0 + preact * (1.0 - sigmas))
    ).astype(jnp.bfloat16)

    pad = terms_ref.shape[0] - (offsets + 1) * channels
    if pad:
        terms_ref[pl.ds((offsets + 1) * channels, pad), :] = jnp.zeros((pad, channels), jnp.bfloat16)

    def term_step(o, carry):
        at = pl.ds(pl.multiple_of(o * channels, channels), channels)
        terms_ref[at, :] = lax.dot_general(
            gathered[at, :], pgrad[...], (((1,), (1,)), ((), ())),
            preferred_element_type=jnp.float32,
        ).astype(jnp.bfloat16)
        return carry

    lax.fori_loop(0, offsets + 1, term_step, 0)

    acc[...] = jnp.zeros_like(acc)

    def scatter_step(j, carry):
        o = j + (j >= center).astype(jnp.int32)
        spread = jnp.dot(weight_ref[o], pgrad[...], preferred_element_type=jnp.float32)
        part = nbr_ref[o] // GROUP
        stacked = jnp.concatenate(
            [jnp.where(part == g, spread, 0.0).astype(jnp.bfloat16) for g in range(groups)], axis=0
        )
        acc[...] += lax.dot_general(
            stacked, onehot[o], (((1,), (1,)), ((), ())), preferred_element_type=jnp.float32
        )
        return carry

    lax.fori_loop(0, offsets - 1, scatter_step, 0)
    spread = jnp.dot(weight_ref[center], pgrad[...], preferred_element_type=jnp.float32)
    own_groups = rows // GROUP
    for g in range(own_groups):
        mine = acc[pl.ds(g * channels, channels), :] + spread[:, g * GROUP : (g + 1) * GROUP]
        own_ref[pl.ds(g * GROUP, GROUP), :] = mine.T
    for g in range(own_groups, groups):
        halo_ref[pl.ds((g - own_groups) * GROUP, GROUP), :] = acc[pl.ds(g * channels, channels), :].T


def brick_pass(extended, matched, offsets_map, label_row, weights, cls_weight, term_rows):
    rows, channels = matched.shape
    offsets = offsets_map.shape[0]
    groups = -(-(extended.shape[0] + 1) // GROUP)
    halo_rows = groups * GROUP - rows
    vmem = pl.BlockSpec(memory_space=pltpu.VMEM)
    return pl.pallas_call(
        functools.partial(brick_kernel, offsets, groups),
        out_shape=(
            jax.ShapeDtypeStruct((rows, channels), jnp.bfloat16),
            jax.ShapeDtypeStruct((rows, channels), jnp.float32),
            jax.ShapeDtypeStruct((halo_rows, channels), jnp.float32),
            jax.ShapeDtypeStruct((term_rows, channels), jnp.bfloat16),
        ),
        in_specs=[vmem] * 6,
        out_specs=(vmem,) * 4,
        scratch_shapes=[
            pltpu.VMEM((groups * channels, GROUP), jnp.bfloat16),
            pltpu.VMEM((offsets, GROUP, rows), jnp.bfloat16),
            pltpu.VMEM(((offsets + 1) * channels, rows), jnp.bfloat16),
            pltpu.VMEM((groups * channels, GROUP), jnp.float32),
            pltpu.VMEM((channels, rows), jnp.bfloat16),
        ],
        compiler_params=pltpu.CompilerParams(vmem_limit_bytes=48 * 1024 * 1024),
        name="brick",
    )(
        extended, matched, offsets_map.reshape(offsets, 1, rows), label_row.reshape(1, rows),
        weights, cls_weight.reshape(channels, 1),
    )


AXES = ("gx", "ta", "gy")


def total_kernel(sizes, x_ref, o_ref, *scratch):
    stages = len(AXES)
    recv, part = scratch[:stages], scratch[stages : 2 * stages]
    send_sem, recv_sem, gsend_sem, grecv_sem = scratch[2 * stages : 2 * stages + 4]
    me = [lax.axis_index(axis) for axis in AXES]
    barrier = pltpu.get_barrier_semaphore()
    for i, axis in enumerate(AXES):
        for k in range(1, sizes[i]):
            pl.semaphore_signal(
                barrier, inc=1, device_id={axis: lax.rem(me[i] + k, sizes[i])}, device_id_type=MESH
            )
    pl.semaphore_wait(barrier, sum(sizes) - stages)
    whole = part[-1]
    source = x_ref
    base = 0
    length = x_ref.shape[0]
    bases = []
    slot = 0
    for i, axis in enumerate(AXES):
        n = sizes[i]
        piece = length // n
        copies = []
        for k in range(1, n):
            peer = lax.rem(me[i] + k, n)
            copy = pltpu.make_async_remote_copy(
                src_ref=source.at[pl.ds(pl.multiple_of(peer * piece, 16), piece)],
                dst_ref=recv[i].at[k - 1],
                send_sem=send_sem.at[slot],
                recv_sem=recv_sem.at[slot],
                device_id={axis: peer},
                device_id_type=MESH,
            )
            copy.start()
            copies.append(copy)
            slot += 1
        total = source[pl.ds(pl.multiple_of(me[i] * piece, 16), piece), :].astype(jnp.float32)
        for k, copy in enumerate(copies):
            copy.wait()
            total += recv[i][k].astype(jnp.float32)
        base = base + me[i] * piece
        length = piece
        bases.append((base, piece))
        if i == stages - 1:
            whole[pl.ds(pl.multiple_of(base, 16), piece), :] = total.astype(jnp.bfloat16)
        else:
            part[i][...] = total.astype(jnp.bfloat16)
            source = part[i]
    slot = 0
    for i in reversed(range(stages)):
        n = sizes[i]
        base, piece = bases[i]
        at = whole.at[pl.ds(pl.multiple_of(base, 16), piece)]
        copies = []
        for k in range(1, n):
            copy = pltpu.make_async_remote_copy(
                src_ref=at,
                dst_ref=at,
                send_sem=gsend_sem.at[slot],
                recv_sem=grecv_sem.at[slot],
                device_id={AXES[i]: lax.rem(me[i] + k, n)},
                device_id_type=MESH,
            )
            copy.start()
            copies.append(copy)
            slot += 1
        for copy in copies:
            copy.wait()
    o_ref[...] = whole[...]


def total_terms(terms):
    rows, channels = terms.shape
    sizes = tuple(lax.axis_size(axis) for axis in AXES)
    vmem = pl.BlockSpec(memory_space=pltpu.VMEM)
    recv, part = [], []
    length = rows
    for n in sizes:
        length //= n
        recv.append(pltpu.VMEM((n - 1, length, channels), jnp.bfloat16))
        part.append(pltpu.VMEM((length, channels), jnp.bfloat16))
    part[-1] = pltpu.VMEM((rows, channels), jnp.bfloat16)
    count = sum(sizes) - len(sizes)
    return pl.pallas_call(
        functools.partial(total_kernel, sizes),
        out_shape=jax.ShapeDtypeStruct((rows, channels), jnp.bfloat16),
        in_specs=[vmem],
        out_specs=vmem,
        scratch_shapes=recv + part + [pltpu.SemaphoreType.DMA((count,))] * 4,
        compiler_params=pltpu.CompilerParams(collective_id=0, has_side_effects=True),
        name="total",
    )(terms)


def per_device(
    feat, ref_feat, rim_rows, nbr, send_blocks, send_count, match_slot, labels,
    conv_weight, ref_weight, cls_weight,
):
    current = feat[0, 0, 0]
    rows, channels = current.shape
    offsets = conv_weight.shape[0]
    rim_index = rim_rows[0, 0, 0]
    rim_count = rim_index.shape[0]
    rim_feat = current[rim_index]
    padded = with_halo(rim_feat[None, None, None], (("gx", 1), ("gy", 2)), 1)
    halo_rows = padded[0].reshape(9 * rim_count, channels)
    extended = jnp.concatenate([current, halo_rows], axis=0)
    routed = route_blocks(pack_blocks(ref_feat[0, 0, 0], send_blocks[0, 0, 0], send_count[0, 0, 0]))
    received = passed_along(routed, "ta", 1)
    table = jnp.concatenate(
        [received.reshape(-1, BLOCK, channels), jnp.zeros((1, BLOCK, channels), jnp.bfloat16)],
        axis=0,
    )
    matched = table[match_slot[0, 0, 0]].reshape(rows, channels)
    weights = jnp.concatenate([conv_weight, ref_weight[None]], axis=0)
    devices = lax.axis_size("ta") * lax.axis_size("gx") * lax.axis_size("gy")
    step = 16 * devices
    term_rows = -(-(offsets + 1) * channels // step) * step
    activ, own_grad, halo_grad, terms = brick_pass(
        extended, matched, nbr[0, 0, 0], labels[0, 0, 0], weights, cls_weight, term_rows
    )
    halo_grad = halo_grad[: 9 * rim_count].reshape(3, 3, rim_count, channels)
    column = halo_grad[1]
    for slot_x in (0, 2):
        column = column + passed_along(
            halo_grad[slot_x].astype(jnp.bfloat16), "gx", slot_x - 1
        ).astype(jnp.float32)
    rim_grad = column[1]
    for slot_y in (0, 2):
        rim_grad = rim_grad + passed_along(column[slot_y], "gy", slot_y - 1)
    spot = (jnp.arange(rows)[:, None] == rim_index[None, :]).astype(jnp.bfloat16)
    feature_grad = (
        own_grad
        + jnp.dot(spot, rim_grad.astype(jnp.bfloat16), preferred_element_type=jnp.float32)
    ).astype(jnp.bfloat16)
    summed = total_terms(terms).astype(jnp.float32)
    weight_grad = summed[: offsets * channels].reshape(offsets, channels, channels)
    ref_grad = summed[offsets * channels : (offsets + 1) * channels]
    return (activ[None, None, None], feature_grad[None, None, None], weight_grad, ref_grad)


def solution(mesh):
    placed = (
        P("ta", "gx", "gy", None, None),
        P("ta", "gx", "gy", None, None),
        P("ta", "gx", "gy", None),
        P("ta", "gx", "gy", None, None),
        P("ta", "gx", "gy", None, None),
        P("ta", "gx", "gy", None),
        P("ta", "gx", "gy", None),
        P("ta", "gx", "gy", None),
        P(),
        P(),
        P(),
    )
    return jax.shard_map(
        per_device,
        mesh=mesh,
        in_specs=placed,
        out_specs=(P("ta", "gx", "gy", None, None), P("ta", "gx", "gy", None, None), P(), P()),
        check_vma=False,
    )
```

time: 422 us -> 127 us (0.30); the launches traced: 418 us -> 127 us
  matrix products: 202 us -> 0.89 us
  waiting for transfers between devices: 130 us -> 17 us
  Pallas kernels: 0 us -> 69.7 us
  local copies, waits for them, and re-layouts: 29.1 us -> 7.07 us
  between operations: 14.4 us -> 1.01 us
  loops' own time: 7.23 us -> 0 us
    dot_general x246 -> x1, matrix products: 202 us -> 0.89 us  [per_device(): jnp.dot(spot, rim_grad.astype(jnp.bfloat16), preferred_element_type=jnp.f...]
    psum x1 -> x0, waiting for transfers between devices: 118 us -> none  [per_device(): lax.psum((weight_terms, ref_term), ('ta', 'gx', 'gy'))]
    pallas_call x0 -> x2, Pallas kernels: none -> 69.7 us  [the longest x1 39.4 us: brick_pass(): pl.pallas_call(functools.partial(brick_kernel, offsets, groups), out_shap...]
    dynamic_update_slice x54 -> x0, local copies, waits for them, and re-layouts: 19.7 us -> none  [per_device(): lax.scan(backward_step, jnp.zeros((ext_rows, channels), jnp.float32), (of...]
    another operation x56 -> x0, loops' own time: 7.23 us -> none  [the longest x27 2.53 us: backward_step(): lax.scan(add_block, jnp.zeros((ext_rows, channels), jnp.float32), (index_...]
    all_to_all x1, waiting for transfers between devices: 4.08 us -> 9.61 us  [route_blocks(): lax.all_to_all(buffer, ('gx', 'gy'), split_axis=0, concat_axis=0, tiled=T...]
  transfers between devices with their start and end apart: 11 -> 10, of which waited for: 6 -> 4; matrix products, arithmetic and copies ran while one was open for 16% -> 4% of each run, Pallas kernels for 0% -> 24%
where the time goes in v1:
time: 127 us
  Pallas kernels  69.7 us (55%)
  starting transfers between devices  28.6 us (23%)
  waiting for transfers between devices  17 us (13%)
  local copies, waits for them, and re-layouts  7.07 us (6%)
  other arithmetic  2.6 us (2%)
    pallas_call x1, Pallas kernels, brick_pass(): pl.pallas_call(functools.partial(brick_kernel, offsets, groups), out_shap...  39.4 us
    pallas_call x1, Pallas kernels, total_terms(): pl.pallas_call(functools.partial(total_kernel, sizes), out_shape=jax.Shap...  30.3 us
    ppermute x5, starting transfers between devices, passed_along(): return lax.ppermute(block, axis, route)  12 us
    all_to_all x1, waiting for transfers between devices, route_blocks(): lax.all_to_all(buffer, ('gx', 'gy'), split_axis=0, concat_axis=0, tiled=T...  9.61 us
    ppermute x2, starting transfers between devices, with_halo(): lax.ppermute(lax.slice_in_dim(block, block.shape[dim] - width, None, axis...  7.58 us
    all_to_all x1, starting transfers between devices, route_blocks(): lax.all_to_all(buffer, ('gx', 'gy'), split_axis=0, concat_axis=0, tiled=T...  6.49 us
    ppermute x5, waiting for transfers between devices, passed_along(): return lax.ppermute(block, axis, route)  5.92 us
    ppermute x2, starting transfers between devices, with_halo(): lax.ppermute(lax.slice_in_dim(block, 0, width, axis=dim), axis, backward)  2.58 us
  transfers between devices with their start and end apart: 10, of which 4 were waited for; matrix products, arithmetic and copies ran while one was open for 4% of the time, Pallas kernels for 24%

profile of v1, /device:TPU:0, one launch (start us, length us, event | category | flops | bytes accessed | tf_op | source)
XLA Modules:
  0.0 126.9 jit_solution(4608293291887275011)
XLA Ops:
  0.6 0.0 copy-start
  0.6 0.0 copy-start.9
  0.7 0.0 copy-start.5
  0.7 0.0 copy-start.10
  0.7 0.0 copy-start.7
  0.7 0.0 copy-start.4
  0.7 0.8 compare_select_fusion
  1.5 0.7 iota_compare_fusion.2
  2.2 0.1 copy.17
  2.3 0.1 reshape.152
  2.4 0.0 copy-done
  2.4 0.6 gather_fusion.1
  3.0 0.9 broadcast_select_fusion
  3.9 0.0 copy-start.8
  4.0 0.0 copy-start.6
  4.0 6.5 %all-to-all-start = ((bf16[8,2,128,128]{3,2,1,0:T(8,128)(2,1)}), bf16[8,2,128,128]{3,2,1,0:T(8,128)(2,1)S(1)}, u32[]{:S(2)}, u32[]{:S(2)}) async-start(bf16[8,2,128,128]{3,2,1,0:T(8,128)(2,1)} %broadcast_select_fusion), calls=%async_computation | async-start | bytes 1048576 | tf_op jit(solution)/shard_map/all_to_all | solution.py:45
  10.4 0.0 copy-done.9
  10.5 0.0 copy-done.5
  10.5 0.6 gather_fusion
  11.1 1.3 %collective-permute-start.1 = (bf16[1,1,1,48,128]{4,3,2,1,0:T(8,128)(2,1)S(1)}, bf16[1,1,1,48,128]{4,3,2,1,0:T(8,128)(2,1)S(1)}, u32[]{:S(2)}, u32[]{:S(2)}) collective-permute-start(bf16[1,1,1,48,128]{4,3,2,1,0:T(8,128)(2,1)S(1)} %bitcast.56), channel_id=1, source_target_pairs={{4,0},{5,1},{6,2},{7,3},{12,8},{13,9},{14,10},{15,11},{20,16},{21,... | collective-permute-start | bytes 36872 | tf_op jit(solution)/shard_map/ppermute | solution.py:25
  12.4 3.0 %collective-permute-start = (bf16[1,1,1,48,128]{4,3,2,1,0:T(8,128)(2,1)S(1)}, bf16[1,1,1,48,128]{4,3,2,1,0:T(8,128)(2,1)S(1)}, u32[]{:S(2)}, u32[]{:S(2)}) collective-permute-start(bf16[1,1,1,48,128]{4,3,2,1,0:T(8,128)(2,1)S(1)} %bitcast.57), channel_id=1, source_target_pairs={{0,4},{1,5},{2,6},{3,7},{8,12},{9,13},{10,14},{11,15},{16,20},{17,... | collective-permute-start | bytes 36872 | tf_op jit(solution)/shard_map/ppermute | solution.py:22
  15.4 0.0 copy-done.10
  15.4 0.0 copy-done.7
  15.5 0.0 copy-done.4
  15.5 0.0 copy-start.2
  15.5 0.0 copy-start.3
  15.5 0.1 pad_maximum_fusion.weight_ref
  15.6 9.6 %all-to-all-done = bf16[8,2,128,128]{3,2,1,0:T(8,128)(2,1)S(1)} async-done(((bf16[8,2,128,128]{3,2,1,0:T(8,128)(2,1)}), bf16[8,2,128,128]{3,2,1,0:T(8,128)(2,1)S(1)}, u32[]{:S(2)}, u32[]{:S(2)}) %all-to-all-start) | async-done | bytes 524320 | tf_op jit(solution)/shard_map/all_to_all | solution.py:45
  25.2 3.4 %collective-permute-start.4 = (bf16[8,2,128,128]{3,2,1,0:T(8,128)(2,1)S(1)}, bf16[8,2,128,128]{3,2,1,0:T(8,128)(2,1)S(1)}, u32[]{:S(2)}, u32[]{:S(2)}) collective-permute-start(bf16[8,2,128,128]{3,2,1,0:T(8,128)(2,1)S(1)} %all-to-all-done), channel_id=1, source_target_pairs={{0,8},{8,16},{16,24},{1,9},{9,17},{17,25},{2,10},{10,18},{18,26},{... | collective-permute-start | bytes 1572872 | tf_op jit(solution)/shard_map/ppermute | solution.py:33
  28.6 0.0 collective-permute-done.1
  28.6 0.0 collective-permute-done
  28.7 1.3 %collective-permute-start.3 = (bf16[1,3,1,48,128]{4,3,2,1,0:T(8,128)(2,1)S(1)}, bf16[1,3,1,48,128]{4,3,2,1,0:T(8,128)(2,1)S(1)}, u32[]{:S(2)}, u32[]{:S(2)}) collective-permute-start(bf16[1,3,1,48,128]{4,3,2,1,0:T(8,128)(2,1)S(1)} %pad_maximum_fusion.3), channel_id=1, source_target_pairs={{1,0},{2,1},{3,2},{5,4},{6,5},{7,6},{9,8},{10,9},{11,10},{13,12},{... | collective-permute-start | bytes 110600 | tf_op jit(solution)/shard_map/ppermute | solution.py:25
  30.0 4.5 %collective-permute-start.2 = (bf16[1,3,1,48,128]{4,3,2,1,0:T(8,128)(2,1)S(1)}, bf16[1,3,1,48,128]{4,3,2,1,0:T(8,128)(2,1)S(1)}, u32[]{:S(2)}, u32[]{:S(2)}) collective-permute-start(bf16[1,3,1,48,128]{4,3,2,1,0:T(8,128)(2,1)S(1)} %pad_maximum_fusion.3), channel_id=1, source_target_pairs={{0,1},{1,2},{2,3},{4,5},{5,6},{6,7},{8,9},{9,10},{10,11},{12,13},{... | collective-permute-start | bytes 110600 | tf_op jit(solution)/shard_map/ppermute | solution.py:22
  34.5 0.0 copy-done.8
  34.5 0.1 copy.18.cls_ref
  34.7 0.0 collective-permute-done.3
  34.7 1.5 %collective-permute-done.2 = bf16[1,3,1,48,128]{4,3,2,1,0:T(8,128)(2,1)S(1)} collective-permute-done((bf16[1,3,1,48,128]{4,3,2,1,0:T(8,128)(2,1)S(1)}, bf16[1,3,1,48,128]{4,3,2,1,0:T(8,128)(2,1)S(1)}, u32[]{:S(2)}, u32[]{:S(2)}) %collective-permute-start.2) | collective-permute-done | bytes 36896 | tf_op jit(solution)/shard_map/ppermute | solution.py:22
  36.1 0.0 copy-done.6
  36.2 4.1 %collective-permute-done.4 = bf16[8,2,128,128]{3,2,1,0:T(8,128)(2,1)S(1)} collective-permute-done((bf16[8,2,128,128]{3,2,1,0:T(8,128)(2,1)S(1)}, bf16[8,2,128,128]{3,2,1,0:T(8,128)(2,1)S(1)}, u32[]{:S(2)}, u32[]{:S(2)}) %collective-permute-start.4) | collective-permute-done | bytes 524320 | tf_op jit(solution)/shard_map/ppermute | solution.py:33
  40.4 0.6 gather_fusion.2
  41.0 0.0 copy-done.2
  41.0 0.0 copy-done.3
  41.0 39.4 %brick.1 = (bf16[768,128]{1,0:T(8,128)(2,1)}, f32[768,128]{1,0:T(8,128)S(1)}, f32[512,128]{1,0:T(8,128)S(1)}, bf16[3584,128]{1,0:T(8,128)(2,1)S(1)}) custom-call(bf16[1200,128]{1,0:T(8,128)(2,1)S(1)} %pad_maximum_fusion.1.ext_ref, bf16[768,128]{1,0:T(8,128)(2,1)S(1)} %bitcast.46, s32[27,1,768]{2,1,0:T(1,128)S(1)} %bitcast.47, s32[1,768]{1,0:T(1,128)S(1)} %bitcast.48, ...), custom_call_target="tpu_custom_call" | custom-call | tf_op jit(solution)/shard_map/brick/pallas_call | solution.py:142
  80.4 0.0 copy-start.1
  80.4 0.9 copy-done.1
  81.3 1.4 %collective-permute-start.6 = (bf16[3,48,128]{2,1,0:T(8,128)(2,1)S(1)}, bf16[3,48,128]{2,1,0:T(8,128)(2,1)S(1)}, u32[]{:S(2)}, u32[]{:S(2)}) collective-permute-start(bf16[3,48,128]{2,1,0:T(8,128)(2,1)S(1)} %bitcast.61), channel_id=1, source_target_pairs={{0,4},{1,5},{2,6},{3,7},{8,12},{9,13},{10,14},{11,15},{16,20},{17,... | collective-permute-start | bytes 110600 | tf_op jit(solution)/shard_map/ppermute | solution.py:33
  82.8 1.3 %collective-permute-start.5 = (bf16[3,48,128]{2,1,0:T(8,128)(2,1)S(1)}, bf16[3,48,128]{2,1,0:T(8,128)(2,1)S(1)}, u32[]{:S(2)}, u32[]{:S(2)}) collective-permute-start(bf16[3,48,128]{2,1,0:T(8,128)(2,1)S(1)} %bitcast.60), channel_id=1, source_target_pairs={{4,0},{5,1},{6,2},{7,3},{12,8},{13,9},{14,10},{15,11},{20,16},{21,... | collective-permute-start | bytes 110600 | tf_op jit(solution)/shard_map/ppermute | solution.py:33
  84.1 0.0 collective-permute-done.6
  84.1 1.8 %collective-permute-done.5 = bf16[3,48,128]{2,1,0:T(8,128)(2,1)S(1)} collective-permute-done((bf16[3,48,128]{2,1,0:T(8,128)(2,1)S(1)}, bf16[3,48,128]{2,1,0:T(8,128)(2,1)S(1)}, u32[]{:S(2)}, u32[]{:S(2)}) %collective-permute-start.5) | collective-permute-done | bytes 36896 | tf_op jit(solution)/shard_map/ppermute | solution.py:33
  85.9 1.3 %collective-permute-start.7 = (f32[48,128]{1,0:T(8,128)S(1)}, f32[48,128]{1,0:T(8,128)S(1)}, u32[]{:S(2)}, u32[]{:S(2)}) collective-permute-start(f32[48,128]{1,0:T(8,128)S(1)} %get-tuple-element.14), channel_id=1, source_target_pairs={{1,0},{2,1},{3,2},{5,4},{6,5},{7,6},{9,8},{10,9},{11,10},{13,12},{... | collective-permute-start | bytes 73736 | tf_op jit(solution)/shard_map/ppermute | solution.py:33
  87.2 4.5 %collective-permute-start.8 = (f32[48,128]{1,0:T(8,128)S(1)}, f32[48,128]{1,0:T(8,128)S(1)}, u32[]{:S(2)}, u32[]{:S(2)}) collective-permute-start(f32[48,128]{1,0:T(8,128)S(1)} %get-tuple-element.15), channel_id=1, source_target_pairs={{0,1},{1,2},{2,3},{4,5},{5,6},{6,7},{8,9},{9,10},{10,11},{12,13},{... | collective-permute-start | bytes 73736 | tf_op jit(solution)/shard_map/ppermute | solution.py:33
  91.8 30.3 %total.1 = bf16[3584,128]{1,0:T(8,128)(2,1)} custom-call(bf16[3584,128]{1,0:T(8,128)(2,1)} %copy-done.1), custom_call_target="tpu_custom_call" | custom-call | tf_op jit(solution)/shard_map/total/pallas_call | solution.py:252
  122.1 1.4 %slice.53 = f32[128,128]{1,0:T(8,128)} slice(bf16[3584,128]{1,0:T(8,128)(2,1)} %total.1), slice={[3456:3584], [0:128]} | slice | bytes 131072 | tf_op jit(solution)/shard_map/slice | solution.py:306
  123.5 2.5 %slice.52 = f32[3456,128]{1,0:T(8,128)} slice(bf16[3584,128]{1,0:T(8,128)(2,1)} %total.1), slice={[0:3456], [0:128]} | slice | bytes 3538944 | tf_op jit(solution)/shard_map/slice | solution.py:305
  126.0 0.0 collective-permute-done.7
  126.0 0.0 collective-permute-done.8
  126.0 0.9 fusion.1
  (14 shorter events, 0.2 us)
Async XLA Ops:
  0.6 1.8 %copy-start = (bf16[1,1,1,768,128]{4,3,2,1,0:T(8,128)(2,1)S(1)}, bf16[1,1,1,768,128]{4,3,2,1,0:T(8,128)(2,1)}, u32[]{:S(2)}) copy-start(bf16[1,1,1,768,128]{4,3,2,1,0:T(8,128)(2,1)} %param.12) | copy-start | bytes 589828
  0.6 9.8 %copy-start.9 = (s32[1,1,1,48]{3,2,1,0:T(1,128)S(1)}, s32[1,1,1,48]{3,2,1,0:T(1,128)}, u32[]{:S(2)}) copy-start(s32[1,1,1,48]{3,2,1,0:T(1,128)} %param.13) | copy-start | bytes 580
  0.7 9.8 %copy-start.5 = (bf16[1,1,1,768,128]{4,3,2,1,0:T(8,128)(2,1)S(1)}, bf16[1,1,1,768,128]{4,3,2,1,0:T(8,128)(2,1)}, u32[]{:S(2)}) copy-start(bf16[1,1,1,768,128]{4,3,2,1,0:T(8,128)(2,1)} %param.11) | copy-start | bytes 589828
  0.7 14.8 %copy-start.10 = (s32[1,1,1,6]{3,2,1,0:T(1,128)S(1)}, s32[1,1,1,6]{3,2,1,0:T(1,128)}, u32[]{:S(2)}) copy-start(s32[1,1,1,6]{3,2,1,0:T(1,128)} %param.17) | copy-start | bytes 76
  0.7 14.8 %copy-start.7 = (bf16[128,128]{1,0:T(8,128)(2,1)S(1)}, bf16[128,128]{1,0:T(8,128)(2,1)}, u32[]{:S(2)}) copy-start(bf16[128,128]{1,0:T(8,128)(2,1)} %param.20) | copy-start | bytes 98308
  0.7 14.8 %copy-start.4 = (bf16[27,128,128]{2,1,0:T(8,128)(2,1)S(1)}, bf16[27,128,128]{2,1,0:T(8,128)(2,1)}, u32[]{:S(2)}) copy-start(bf16[27,128,128]{2,1,0:T(8,128)(2,1)} %param.19) | copy-start | bytes 2654212
  3.9 30.6 %copy-start.8 = (bf16[128]{0:T(256)(128)(2,1)S(1)}, bf16[128]{0:T(256)(128)(2,1)}, u32[]{:S(2)}) copy-start(bf16[128]{0:T(256)(128)(2,1)} %param.21) | copy-start | bytes 772
  4.0 32.2 %copy-start.6 = (bf16[1,1,1,768,128]{4,3,2,1,0:T(8,128)(2,1)S(1)}, bf16[1,1,1,768,128]{4,3,2,1,0:T(8,128)(2,1)}, u32[]{:S(2)}) copy-start(bf16[1,1,1,768,128]{4,3,2,1,0:T(8,128)(2,1)} %param.11) | copy-start | bytes 589828
  4.0 21.2 %all-to-all-start = ((bf16[8,2,128,128]{3,2,1,0:T(8,128)(2,1)}), bf16[8,2,128,128]{3,2,1,0:T(8,128)(2,1)S(1)}, u32[]{:S(2)}, u32[]{:S(2)}) async-start(bf16[8,2,128,128]{3,2,1,0:T(8,128)(2,1)} %broadcast_select_fusion), calls=%async_computation | async-start | bytes 1048576 | tf_op jit(solution)/shard_map/all_to_all | solution.py:45
  11.1 17.5 %collective-permute-start.1 = (bf16[1,1,1,48,128]{4,3,2,1,0:T(8,128)(2,1)S(1)}, bf16[1,1,1,48,128]{4,3,2,1,0:T(8,128)(2,1)S(1)}, u32[]{:S(2)}, u32[]{:S(2)}) collective-permute-start(bf16[1,1,1,48,128]{4,3,2,1,0:T(8,128)(2,1)S(1)} %bitcast.56), channel_id=1, source_target_pairs={{4,0},{5,1},{6,2},{7,3},{12,8},{13,9},{14,10},{15,11},{20,16},{21,... | collective-permute-start | bytes 36872 | tf_op jit(solution)/shard_map/ppermute | solution.py:25
  12.4 16.2 %collective-permute-start = (bf16[1,1,1,48,128]{4,3,2,1,0:T(8,128)(2,1)S(1)}, bf16[1,1,1,48,128]{4,3,2,1,0:T(8,128)(2,1)S(1)}, u32[]{:S(2)}, u32[]{:S(2)}) collective-permute-start(bf16[1,1,1,48,128]{4,3,2,1,0:T(8,128)(2,1)S(1)} %bitcast.57), channel_id=1, source_target_pairs={{0,4},{1,5},{2,6},{3,7},{8,12},{9,13},{10,14},{11,15},{16,20},{17,... | collective-permute-start | bytes 36872 | tf_op jit(solution)/shard_map/ppermute | solution.py:22
  15.5 25.5 %copy-start.2 = (s32[1,1,1,27,768]{4,2,3,1,0:T(1,128)S(1)}, s32[1,1,1,27,768]{4,2,3,1,0:T(1,128)}, u32[]{:S(2)}) copy-start(s32[1,1,1,27,768]{4,2,3,1,0:T(1,128)} %param.14) | copy-start | bytes 248836
  15.5 25.5 %copy-start.3 = (s32[1,1,1,768]{3,2,1,0:T(1,128)S(1)}, s32[1,1,1,768]{3,2,1,0:T(1,128)}, u32[]{:S(2)}) copy-start(s32[1,1,1,768]{3,2,1,0:T(1,128)} %param.18) | copy-start | bytes 9220
  25.2 15.1 %collective-permute-start.4 = (bf16[8,2,128,128]{3,2,1,0:T(8,128)(2,1)S(1)}, bf16[8,2,128,128]{3,2,1,0:T(8,128)(2,1)S(1)}, u32[]{:S(2)}, u32[]{:S(2)}) collective-permute-start(bf16[8,2,128,128]{3,2,1,0:T(8,128)(2,1)S(1)} %all-to-all-done), channel_id=1, source_target_pairs={{0,8},{8,16},{16,24},{1,9},{9,17},{17,25},{2,10},{10,18},{18,26},{... | collective-permute-start | bytes 1572872 | tf_op jit(solution)/shard_map/ppermute | solution.py:33
  28.7 6.0 %collective-permute-start.3 = (bf16[1,3,1,48,128]{4,3,2,1,0:T(8,128)(2,1)S(1)}, bf16[1,3,1,48,128]{4,3,2,1,0:T(8,128)(2,1)S(1)}, u32[]{:S(2)}, u32[]{:S(2)}) collective-permute-start(bf16[1,3,1,48,128]{4,3,2,1,0:T(8,128)(2,1)S(1)} %pad_maximum_fusion.3), channel_id=1, source_target_pairs={{1,0},{2,1},{3,2},{5,4},{6,5},{7,6},{9,8},{10,9},{11,10},{13,12},{... | collective-permute-start | bytes 110600 | tf_op jit(solution)/shard_map/ppermute | solution.py:25
  30.0 6.2 %collective-permute-start.2 = (bf16[1,3,1,48,128]{4,3,2,1,0:T(8,128)(2,1)S(1)}, bf16[1,3,1,48,128]{4,3,2,1,0:T(8,128)(2,1)S(1)}, u32[]{:S(2)}, u32[]{:S(2)}) collective-permute-start(bf16[1,3,1,48,128]{4,3,2,1,0:T(8,128)(2,1)S(1)} %pad_maximum_fusion.3), channel_id=1, source_target_pairs={{0,1},{1,2},{2,3},{4,5},{5,6},{6,7},{8,9},{9,10},{10,11},{12,13},{... | collective-permute-start | bytes 110600 | tf_op jit(solution)/shard_map/ppermute | solution.py:22
  80.4 0.9 copy-start.1
  81.3 2.8 %collective-permute-start.6 = (bf16[3,48,128]{2,1,0:T(8,128)(2,1)S(1)}, bf16[3,48,128]{2,1,0:T(8,128)(2,1)S(1)}, u32[]{:S(2)}, u32[]{:S(2)}) collective-permute-start(bf16[3,48,128]{2,1,0:T(8,128)(2,1)S(1)} %bitcast.61), channel_id=1, source_target_pairs={{0,4},{1,5},{2,6},{3,7},{8,12},{9,13},{10,14},{11,15},{16,20},{17,... | collective-permute-start | bytes 110600 | tf_op jit(solution)/shard_map/ppermute | solution.py:33
  82.8 3.1 %collective-permute-start.5 = (bf16[3,48,128]{2,1,0:T(8,128)(2,1)S(1)}, bf16[3,48,128]{2,1,0:T(8,128)(2,1)S(1)}, u32[]{:S(2)}, u32[]{:S(2)}) collective-permute-start(bf16[3,48,128]{2,1,0:T(8,128)(2,1)S(1)} %bitcast.60), channel_id=1, source_target_pairs={{4,0},{5,1},{6,2},{7,3},{12,8},{13,9},{14,10},{15,11},{20,16},{21,... | collective-permute-start | bytes 110600 | tf_op jit(solution)/shard_map/ppermute | solution.py:33
  85.9 40.0 %collective-permute-start.7 = (f32[48,128]{1,0:T(8,128)S(1)}, f32[48,128]{1,0:T(8,128)S(1)}, u32[]{:S(2)}, u32[]{:S(2)}) collective-permute-start(f32[48,128]{1,0:T(8,128)S(1)} %get-tuple-element.14), channel_id=1, source_target_pairs={{1,0},{2,1},{3,2},{5,4},{6,5},{7,6},{9,8},{10,9},{11,10},{13,12},{... | collective-permute-start | bytes 73736 | tf_op jit(solution)/shard_map/ppermute | solution.py:33
  87.2 38.7 %collective-permute-start.8 = (f32[48,128]{1,0:T(8,128)S(1)}, f32[48,128]{1,0:T(8,128)S(1)}, u32[]{:S(2)}, u32[]{:S(2)}) collective-permute-start(f32[48,128]{1,0:T(8,128)S(1)} %get-tuple-element.15), channel_id=1, source_target_pairs={{0,1},{1,2},{2,3},{4,5},{5,6},{6,7},{8,9},{9,10},{10,11},{12,13},{... | collective-permute-start | bytes 73736 | tf_op jit(solution)/shard_map/ppermute | solution.py:33

commit v2 on v0

v2 whole, which is shorter than its diff:
```python
import functools

import jax
import jax.numpy as jnp
from jax import lax
from jax.experimental import pallas as pl
from jax.experimental.pallas import tpu as pltpu
from jax.sharding import PartitionSpec as P

BLOCK = 128
GROUP = 256
MESH = pl.DeviceIdType.MESH
AXES = ("gx", "ta", "gy")

loss_scale = 16.0


def aligned(start, size):
    return pl.ds(pl.multiple_of(start, 16), size)


def step_kernel(
    sizes, cap, rim_count,
    feat_ref, ref_feat_ref, rim_ref, nbr_ref, lists_ref, counts_ref, match_ref, labels_ref,
    weight_ref, ref_weight_ref, cls_ref,
    activ_ref, fgrad_ref, wsum_ref, rsum_ref,
    table, onehot, gathered, acc, pgrad, terms, rim, rims, outbox, inbox, gbox, gin,
    recv_x, recv_t, recv_y, part_x, part_t, whole,
    rim_send, rim_recv, box_send, box_recv, g_send, g_recv, rs_send, rs_recv, ag_send, ag_recv,
):
    offsets = weight_ref.shape[0]
    rows, channels = feat_ref.shape
    groups = table.shape[0] // channels
    own_groups = rows // GROUP
    center = offsets // 2
    pairs = offsets // 2
    n_x, n_t, n_y = sizes["gx"], sizes["ta"], sizes["gy"]
    bricks = n_x * n_y
    x, t, y = lax.axis_index("gx"), lax.axis_index("ta"), lax.axis_index("gy")
    me = {"gx": x, "ta": t, "gy": y}
    q = x * n_y + y

    around = [(dx, dy) for dx in (-1, 0, 1) for dy in (-1, 0, 1) if (dx, dy) != (0, 0)]

    def inside(dx, dy):
        return (x + dx >= 0) & (x + dx < n_x) & (y + dy >= 0) & (y + dy < n_y)

    def slot_of(dx, dy):
        return (dx + 1) * 3 + dy + 1

    for dx, dy in around:

        @pl.when(jnp.logical_not(inside(dx, dy)))
        def _():
            n = slot_of(dx, dy)
            rims[pl.ds(n * rim_count, rim_count), :] = jnp.zeros((rim_count, channels), jnp.bfloat16)
            gin[n] = jnp.zeros((rim_count, channels), jnp.bfloat16)

    barrier = pltpu.get_barrier_semaphore()
    for axis in AXES:
        for k in range(1, sizes[axis]):
            pl.semaphore_signal(
                barrier, inc=1, device_id={axis: lax.rem(me[axis] + k, sizes[axis])},
                device_id_type=MESH,
            )
    for dx, dy in around:
        if dx and dy:

            @pl.when(inside(dx, dy))
            def _():
                pl.semaphore_signal(
                    barrier, inc=1, device_id={"gx": x + dx, "gy": y + dy}, device_id_type=MESH
                )

    @pl.when(t > 0)
    def _():
        for d in range(bricks):
            pl.semaphore_signal(
                barrier, inc=1, device_id={"ta": t - 1, "gx": d // n_y, "gy": d % n_y},
                device_id_type=MESH,
            )

    spot = (lax.broadcasted_iota(jnp.int32, (rows, rim_count), 0) == rim_ref[...]).astype(
        jnp.float32
    ).astype(jnp.bfloat16)
    mine = lax.dot_general(
        spot, feat_ref[...], (((0,), (0,)), ((), ())), preferred_element_type=jnp.float32
    ).astype(jnp.bfloat16)
    rim[...] = mine
    rims[pl.ds(4 * rim_count, rim_count), :] = mine

    sides_x = (x > 0).astype(jnp.int32) + (x < n_x - 1).astype(jnp.int32)
    sides_y = (y > 0).astype(jnp.int32) + (y < n_y - 1).astype(jnp.int32)
    ahead = (t < n_t - 1).astype(jnp.int32)
    pl.semaphore_wait(barrier, n_x + n_t + n_y - 3 + sides_x * sides_y + ahead * bricks)

    def rim_copy(dx, dy, arriving):
        n = slot_of(dx, dy)
        there = n if arriving else 8 - n
        return pltpu.make_async_remote_copy(
            src_ref=rim,
            dst_ref=rims.at[pl.ds(there * rim_count, rim_count)],
            send_sem=rim_send.at[n],
            recv_sem=rim_recv.at[there],
            device_id={"gx": x + dx, "gy": y + dy},
            device_id_type=MESH,
        )

    for dx, dy in around:

        @pl.when(inside(dx, dy))
        def _():
            rim_copy(dx, dy, False).start()

    def box_copy(k, arriving):
        d = lax.rem(q + k, bricks)
        return pltpu.make_async_remote_copy(
            src_ref=outbox.at[d],
            dst_ref=inbox.at[lax.rem(q + bricks - k, bricks) if arriving else q],
            send_sem=box_send.at[k],
            recv_sem=box_recv.at[k],
            device_id={"ta": lax.rem(t + 1, n_t), "gx": d // n_y, "gy": lax.rem(d, n_y)},
            device_id_type=MESH,
        )

    @pl.when(t < n_t - 1)
    def _():
        for d in range(bricks):
            for s in range(cap):
                block = ref_feat_ref[lists_ref[d * cap + s]]
                outbox[d, s] = jnp.where(s < counts_ref[d], block, jnp.zeros_like(block))
        for k in range(bricks):
            box_copy(k, False).start()

    table[...] = jnp.zeros_like(table)
    for g in range(own_groups):
        table[pl.ds(g * channels, channels), :] = feat_ref[pl.ds(g * GROUP, GROUP), :].T
    gathered[pl.ds(center * channels, channels), :] = feat_ref[...].T

    for dx, dy in around:

        @pl.when(inside(dx, dy))
        def _():
            rim_copy(dx, dy, True).wait_recv()

    halo_rows = 9 * rim_count
    for g in range(own_groups, groups):
        start = (g - own_groups) * GROUP
        width = min(GROUP, halo_rows - start)
        if width > 0:
            table[pl.ds(g * channels, channels), pl.ds(0, width)] = rims[pl.ds(start, width), :].T

    slot = lax.broadcasted_iota(jnp.int32, (GROUP, rows), 0)

    def at(o):
        return pl.ds(pl.multiple_of(o * channels, channels), channels)

    def pick(o):
        index = nbr_ref[pl.ds(o, 1), :]
        hit = (slot == (index & (GROUP - 1))).astype(jnp.float32).astype(jnp.bfloat16)
        onehot[o] = hit
        wide = jnp.dot(table[...], hit, preferred_element_type=jnp.float32)
        part = index // GROUP
        picked = wide[:channels]
        for g in range(1, groups):
            picked = jnp.where(part == g, wide[g * channels : (g + 1) * channels], picked)
        picked = picked.astype(jnp.bfloat16)
        gathered[at(o), :] = picked
        return picked

    def times(first, second, left, right):
        weights = jnp.concatenate([first, second], axis=0)
        return lax.dot_general(
            weights, jnp.concatenate([left, right], axis=0), (((0,), (0,)), ((), ())),
            preferred_element_type=jnp.float32,
        )

    def gather_step(j, total):
        o, p = j, j + center + 1
        return total + times(weight_ref[o], weight_ref[p], pick(o), pick(p))

    preact = lax.fori_loop(0, pairs, gather_step, jnp.zeros((channels, rows), jnp.float32))

    @pl.when(t > 0)
    def _():
        for k in range(bricks):
            box_copy(k, True).wait_recv()

    for k in range(rows // BLOCK):
        where = match_ref[k]
        live = (where < bricks * cap) & (t > 0)
        safe = jnp.minimum(where, bricks * cap - 1)
        block = inbox[safe // cap, lax.rem(safe, cap)]
        block = jnp.where(live, block, jnp.zeros_like(block))
        gathered[pl.ds(offsets * channels, channels), pl.ds(k * BLOCK, BLOCK)] = block.T

    preact += times(
        weight_ref[center], ref_weight_ref[...],
        gathered[pl.ds(center * channels, channels), :],
        gathered[pl.ds(offsets * channels, channels), :],
    )
    sigmas = jax.nn.sigmoid(preact)
    activ = (preact * sigmas).astype(jnp.bfloat16)
    scale = jnp.broadcast_to(cls_ref[...].astype(jnp.float32), (channels, channels)).T[:, :1]
    logits = jnp.sum(activ.astype(jnp.float32) * scale, axis=0, keepdims=True)
    resid = jax.nn.sigmoid(logits) - labels_ref[...].astype(jnp.float32)
    pgrad[...] = (
        loss_scale * resid * scale * sigmas * (1.0 + preact * (1.0 - sigmas))
    ).astype(jnp.bfloat16)

    pad = terms.shape[0] - (offsets + 1) * channels
    if pad:
        terms[pl.ds((offsets + 1) * channels, pad), :] = jnp.zeros((pad, channels), jnp.bfloat16)
    chunk = 4 * channels

    def term_step(j, carry):
        here = pl.ds(pl.multiple_of(j * chunk, chunk), chunk)
        terms[here, :] = lax.dot_general(
            gathered[here, :], pgrad[...], (((1,), (1,)), ((), ())),
            preferred_element_type=jnp.float32,
        ).astype(jnp.bfloat16)
        return carry

    lax.fori_loop(0, (offsets + 1) // 4, term_step, 0)

    recv = {"gx": recv_x, "ta": recv_t, "gy": recv_y}
    source = {"gx": terms, "ta": part_x, "gy": part_t}
    first = {"gx": 0, "ta": n_x - 1, "gy": n_x + n_t - 2}
    piece, base = {}, {}
    length, start = terms.shape[0], 0
    for axis in AXES:
        length //= sizes[axis]
        start = start + me[axis] * length
        piece[axis], base[axis] = length, start

    def rs_copy(axis, k):
        peer = lax.rem(me[axis] + k, sizes[axis])
        return pltpu.make_async_remote_copy(
            src_ref=source[axis].at[aligned(peer * piece[axis], piece[axis])],
            dst_ref=recv[axis].at[k - 1],
            send_sem=rs_send.at[first[axis] + k - 1],
            recv_sem=rs_recv.at[first[axis] + k - 1],
            device_id={axis: peer},
            device_id_type=MESH,
        )

    def rs_start(axis):
        for k in range(1, sizes[axis]):
            rs_copy(axis, k).start()

    def rs_finish(axis):
        total = source[axis][aligned(me[axis] * piece[axis], piece[axis]), :].astype(jnp.float32)
        for k in range(1, sizes[axis]):
            rs_copy(axis, k).wait()
            total += recv[axis][k - 1].astype(jnp.float32)
        return total.astype(jnp.bfloat16)

    def ag_copy(axis, k):
        here = whole.at[aligned(base[axis], piece[axis])]
        return pltpu.make_async_remote_copy(
            src_ref=here,
            dst_ref=here,
            send_sem=ag_send.at[first[axis] + k - 1],
            recv_sem=ag_recv.at[first[axis] + k - 1],
            device_id={axis: lax.rem(me[axis] + k, sizes[axis])},
            device_id_type=MESH,
        )

    def ag_start(axis):
        for k in range(1, sizes[axis]):
            ag_copy(axis, k).start()

    def ag_finish(axis):
        for k in range(1, sizes[axis]):
            ag_copy(axis, k).wait()

    rs_start("gx")
    activ_ref[...] = activ.T
    acc[...] = jnp.zeros_like(acc)

    def scatter_step(j, carry):
        o, p = j, j + center + 1
        spread = jnp.dot(
            jnp.concatenate([weight_ref[o], weight_ref[p]], axis=0), pgrad[...],
            preferred_element_type=jnp.float32,
        )
        total = acc[...]
        for i, n in enumerate((o, p)):
            part = nbr_ref[pl.ds(n, 1), :] // GROUP
            values = spread[i * channels : (i + 1) * channels]
            stacked = jnp.concatenate(
                [jnp.where(part == g, values, 0.0).astype(jnp.bfloat16) for g in range(groups)],
                axis=0,
            )
            total += lax.dot_general(
                stacked, onehot[n], (((1,), (1,)), ((), ())), preferred_element_type=jnp.float32
            )
        acc[...] = total
        return carry

    early, late = pairs // 4, (pairs * 2) // 3
    lax.fori_loop(0, early, scatter_step, 0)
    part_x[...] = rs_finish("gx")
    rs_start("ta")
    lax.fori_loop(early, late, scatter_step, 0)
    part_t[...] = rs_finish("ta")
    rs_start("gy")
    lax.fori_loop(late, pairs, scatter_step, 0)

    for dx in (-1, 0, 1):
        for dy in (-1, 0, 1):
            n = slot_of(dx, dy)
            for g in range(own_groups, groups):
                low = max(n * rim_count, (g - own_groups) * GROUP)
                high = min((n + 1) * rim_count, (g - own_groups + 1) * GROUP)
                if low < high:
                    off = low - (g - own_groups) * GROUP
                    gbox[n, pl.ds(low - n * rim_count, high - low), :] = (
                        acc[pl.ds(g * channels, channels), :].T[off : off + high - low]
                    ).astype(jnp.bfloat16)

    def grad_copy(dx, dy, arriving):
        n = slot_of(dx, dy)
        there = n if arriving else 8 - n
        return pltpu.make_async_remote_copy(
            src_ref=gbox.at[n],
            dst_ref=gin.at[there],
            send_sem=g_send.at[n],
            recv_sem=g_recv.at[there],
            device_id={"gx": x + dx, "gy": y + dy},
            device_id_type=MESH,
        )

    for dx, dy in around:

        @pl.when(inside(dx, dy))
        def _():
            grad_copy(dx, dy, False).start()

    whole[aligned(base["gy"], piece["gy"]), :] = rs_finish("gy")
    ag_start("gy")
    spread = jnp.dot(weight_ref[center], pgrad[...], preferred_element_type=jnp.float32)
    for dx, dy in around:

        @pl.when(inside(dx, dy))
        def _():
            grad_copy(dx, dy, True).wait_recv()

    rim_grad = gbox[4].astype(jnp.float32)
    for dx, dy in around:
        rim_grad += gin[slot_of(dx, dy)].astype(jnp.float32)
    added = jnp.dot(spot, rim_grad.astype(jnp.bfloat16), preferred_element_type=jnp.float32)
    for g in range(own_groups):
        here = slice(g * GROUP, (g + 1) * GROUP)
        own = (acc[pl.ds(g * channels, channels), :] + spread[:, here]).T
        fgrad_ref[pl.ds(g * GROUP, GROUP), :] = (own + added[here]).astype(jnp.bfloat16)
    ag_finish("gy")
    ag_start("ta")
    ag_finish("ta")
    ag_start("gx")
    for dx, dy in around:

        @pl.when(inside(dx, dy))
        def _():
            rim_copy(dx, dy, False).wait_send()
            grad_copy(dx, dy, False).wait_send()

    @pl.when(t < n_t - 1)
    def _():
        for k in range(bricks):
            box_copy(k, False).wait_send()

    ag_finish("gx")
    wsum_ref[...] = whole[pl.ds(0, offsets * channels), :]
    rsum_ref[...] = whole[pl.ds(offsets * channels, channels), :]


def per_device(
    feat, ref_feat, rim_rows, nbr, send_blocks, send_count, match_slot, labels,
    conv_weight, ref_weight, cls_weight,
):
    rows, channels = feat.shape[3:]
    offsets = conv_weight.shape[0]
    bricks, cap = send_blocks.shape[3:]
    rim_count = rim_rows.shape[3]
    sizes = {axis: lax.axis_size(axis) for axis in AXES}
    devices = sizes["ta"] * sizes["gx"] * sizes["gy"]
    step = 16 * devices
    term_rows = -(-(offsets + 1) * channels // step) * step
    groups = -(-(rows + 9 * rim_count + 1) // GROUP)
    vmem = pl.BlockSpec(memory_space=pltpu.VMEM)
    smem = pl.BlockSpec(memory_space=pltpu.SMEM)
    recv, part = [], []
    length = term_rows
    for axis in AXES:
        length //= sizes[axis]
        recv.append(pltpu.VMEM((sizes[axis] - 1, length, channels), jnp.bfloat16))
        part.append(pltpu.VMEM((length, channels), jnp.bfloat16))
    part[-1] = pltpu.VMEM((term_rows, channels), jnp.bfloat16)
    peers = sum(sizes.values()) - 3
    dma = pltpu.SemaphoreType.DMA
    activ, fgrad, wsum, rsum = pl.pallas_call(
        functools.partial(step_kernel, sizes, cap, rim_count),
        out_shape=(
            jax.ShapeDtypeStruct((rows, channels), jnp.bfloat16),
            jax.ShapeDtypeStruct((rows, channels), jnp.bfloat16),
            jax.ShapeDtypeStruct((offsets * channels, channels), jnp.bfloat16),
            jax.ShapeDtypeStruct((channels, channels), jnp.bfloat16),
        ),
        in_specs=[vmem, vmem, vmem, vmem, smem, smem, smem, vmem, vmem, vmem, vmem],
        out_specs=(vmem,) * 4,
        scratch_shapes=[
            pltpu.VMEM((groups * channels, GROUP), jnp.bfloat16),
            pltpu.VMEM((offsets, GROUP, rows), jnp.bfloat16),
            pltpu.VMEM(((offsets + 1) * channels, rows), jnp.bfloat16),
            pltpu.VMEM((groups * channels, GROUP), jnp.float32),
            pltpu.VMEM((channels, rows), jnp.bfloat16),
            pltpu.VMEM((term_rows, channels), jnp.bfloat16),
            pltpu.VMEM((rim_count, channels), jnp.bfloat16),
            pltpu.VMEM((9 * rim_count, channels), jnp.bfloat16),
            pltpu.VMEM((bricks, cap, BLOCK, channels), jnp.bfloat16),
            pltpu.VMEM((bricks, cap, BLOCK, channels), jnp.bfloat16),
            pltpu.VMEM((9, rim_count, channels), jnp.bfloat16),
            pltpu.VMEM((9, rim_count, channels), jnp.bfloat16),
            *recv,
            *part,
            dma((9,)), dma((9,)), dma((bricks,)), dma((bricks,)), dma((9,)), dma((9,)),
            dma((peers,)), dma((peers,)), dma((peers,)), dma((peers,)),
        ],
        compiler_params=pltpu.CompilerParams(
            collective_id=0, has_side_effects=True, vmem_limit_bytes=52 * 1024 * 1024
        ),
        name="step",
    )(
        feat.reshape(rows, channels),
        ref_feat.reshape(rows // BLOCK, BLOCK, channels),
        rim_rows.reshape(1, rim_count),
        nbr.reshape(offsets, rows),
        send_blocks.reshape(bricks * cap),
        send_count.reshape(bricks),
        match_slot.reshape(rows // BLOCK),
        labels.reshape(1, rows),
        conv_weight,
        ref_weight,
        cls_weight.reshape(1, channels),
    )
    whole = (1, 1, 1, rows, channels)
    weight_grad = wsum.astype(jnp.float32).reshape(offsets, channels, channels)
    return activ.reshape(whole), fgrad.reshape(whole), weight_grad, rsum.astype(jnp.float32)


def solution(mesh):
    placed = (
        P("ta", "gx", "gy", None, None),
        P("ta", "gx", "gy", None, None),
        P("ta", "gx", "gy", None),
        P("ta", "gx", "gy", None, None),
        P("ta", "gx", "gy", None, None),
        P("ta", "gx", "gy", None),
        P("ta", "gx", "gy", None),
        P("ta", "gx", "gy", None),
        P(),
        P(),
        P(),
    )
    return jax.shard_map(
        per_device,
        mesh=mesh,
        in_specs=placed,
        out_specs=(P("ta", "gx", "gy", None, None), P("ta", "gx", "gy", None, None), P(), P()),
        check_vma=False,
    )
```

time: 422 us -> 68.1 us (0.16)
  matrix products: 202 us -> 0 us
  waiting for transfers between devices: 130 us -> 0 us
  Pallas kernels: 0 us -> 56 us
  starting transfers between devices: 29.5 us -> 0 us
  local copies, waits for them, and re-layouts: 29.1 us -> 9 us
  between operations: 14.4 us -> 0.65 us
  loops' own time: 7.23 us -> 0 us
    dot_general x246 -> x0, matrix products: 202 us -> none  [the longest x81 60.4 us: add_block(): lax.dot_general(selector(index_block, ext_rows), grad_block, (((0,), (0,)...]
    psum x1 -> x0, waiting for transfers between devices: 118 us -> none  [per_device(): lax.psum((weight_terms, ref_term), ('ta', 'gx', 'gy'))]
    pallas_call x0 -> x1, Pallas kernels: none -> 56 us  [per_device(): pl.pallas_call(functools.partial(step_kernel, sizes, cap, rim_count), out...]
    ppermute x9 -> x0, starting transfers between devices: 23.1 us -> none  [the longest x5 13 us: passed_along(): return lax.ppermute(block, axis, route)]
    dynamic_update_slice x54 -> x0, local copies, waits for them, and re-layouts: 19.7 us -> none  [per_device(): lax.scan(backward_step, jnp.zeros((ext_rows, channels), jnp.float32), (of...]
    ppermute x9 -> x0, waiting for transfers between devices: 7.58 us -> none  [the longest x5 3.32 us: passed_along(): return lax.ppermute(block, axis, route)]
    another operation x56 -> x0, loops' own time: 7.23 us -> none  [the longest x27 2.53 us: backward_step(): lax.scan(add_block, jnp.zeros((ext_rows, channels), jnp.float32), (index_...]
    all_to_all x1 -> x0, starting transfers between devices: 6.35 us -> none  [route_blocks(): lax.all_to_all(buffer, ('gx', 'gy'), split_axis=0, concat_axis=0, tiled=T...]
  transfers between devices with their start and end apart: 11 -> 0, of which waited for: 6 -> 0; matrix products, arithmetic and copies ran while one was open for 16% -> 0% of each run, Pallas kernels for 0% -> 0%
where the time goes in v2:
time: 68.1 us; the launch traced here: 67.7 us
  Pallas kernels  56 us (82%)
  local copies, waits for them, and re-layouts  9 us (13%)
  other arithmetic  2.03 us (3%)
    pallas_call x1, Pallas kernels, per_device(): pl.pallas_call(functools.partial(step_kernel, sizes, cap, rim_count), out...  56 us
    unnamed x20, local copies, waits for them, and re-layouts  8.92 us
    reshape x1, other arithmetic, per_device(): weight_grad = wsum.astype(jnp.float32).reshape(offsets, channels, channels)  1.4 us

profile of v2, /device:TPU:0, one launch (start us, length us, event | category | flops | bytes accessed | tf_op | source)
XLA Modules:
  0.0 67.7 jit_solution(6024713328141114883)
XLA Ops:
  0.6 0.9 %copy.19 = s32[1,1,1,27,768]{4,3,2,1,0:T(8,128)S(1)} copy(s32[1,1,1,27,768]{4,2,3,1,0:T(1,128)} %param.14) | data formatting | bytes 165888
  1.5 0.8 %copy.16 = s32[1,1,1,8,2]{4,3,2,1,0:T(8,128)S(1)} copy(s32[1,1,1,8,2]{3,4,2,1,0:T(2,128)} %param.15) | data formatting | bytes 128 | tf_op args[4]
  2.3 0.1 reshape.51.lists_ref
  2.4 0.0 copy-start
  2.4 0.9 %copy-done = bf16[1,1,1,768,128]{4,3,2,1,0:T(8,128)(2,1)S(1)} copy-done((bf16[1,1,1,768,128]{4,3,2,1,0:T(8,128)(2,1)S(1)}, bf16[1,1,1,768,128]{4,3,2,1,0:T(8,128)(2,1)}, u32[]{:S(2)}) %copy-start) | copy-done | bytes 196632
  3.3 0.0 copy-start.1
  3.3 0.9 %copy-done.1 = bf16[1,1,1,768,128]{4,3,2,1,0:T(8,128)(2,1)S(1)} copy-done((bf16[1,1,1,768,128]{4,3,2,1,0:T(8,128)(2,1)S(1)}, bf16[1,1,1,768,128]{4,3,2,1,0:T(8,128)(2,1)}, u32[]{:S(2)}) %copy-start.1) | copy-done | bytes 196632
  4.2 0.0 copy-start.2
  4.2 0.8 %copy-done.2 = bf16[128,128]{1,0:T(8,128)(2,1)S(1)} copy-done((bf16[128,128]{1,0:T(8,128)(2,1)S(1)}, bf16[128,128]{1,0:T(8,128)(2,1)}, u32[]{:S(2)}) %copy-start.2) | copy-done | bytes 32792
  5.0 0.0 copy-start.3
  5.0 0.7 %copy-done.3 = s32[1,1,1,768]{3,2,1,0:T(1,128)S(1)} copy-done((s32[1,1,1,768]{3,2,1,0:T(1,128)S(1)}, s32[1,1,1,768]{3,2,1,0:T(1,128)}, u32[]{:S(2)}) %copy-start.3) | copy-done | bytes 3096
  5.7 0.0 copy-start.4
  5.7 0.7 copy-done.4
  6.3 0.0 copy-start.5
  6.3 0.7 copy-done.5
  7.0 0.0 copy-start.6
  7.0 0.7 copy-done.6
  7.6 0.0 copy-start.7
  7.6 0.7 copy-done.7
  8.3 56.0 %step.1 = (bf16[768,128]{1,0:T(8,128)(2,1)S(1)}, bf16[768,128]{1,0:T(8,128)(2,1)S(1)}, bf16[3456,128]{1,0:T(8,128)(2,1)S(1)}, bf16[128,128]{1,0:T(8,128)(2,1)S(1)}) custom-call(bf16[768,128]{1,0:T(8,128)(2,1)S(1)} %bitcast.20, bf16[6,128,128]{2,1,0:T(8,128)(2,1)S(1)} %bitcast.21, s32[1,48]{1,0:T(1,128)S(1)} %bitcast.23, s32[27,768]{1,0:T(8,128)S(1)} %bitcast.17, ...), custom_call_target="tpu_custom_call" | custom-call | tf_op jit(solution)/shard_map/step/pallas_call | solution.py:402
  64.3 1.4 %convert.1 = f32[27,128,128]{2,1,0:T(8,128)} convert(bf16[27,128,128]{2,1,0:T(8,128)(2,1)S(1)} %bitcast.16) | non-fusion elementwise | flops 442368 | bytes 2654208 | tf_op jit(solution)/shard_map/reshape | solution.py:448
  65.7 0.6 convert_element_type.4
  66.4 0.7 copy.22
  67.1 0.7 copy.23
Async XLA Ops:
  2.4 0.9 %copy-start = (bf16[1,1,1,768,128]{4,3,2,1,0:T(8,128)(2,1)S(1)}, bf16[1,1,1,768,128]{4,3,2,1,0:T(8,128)(2,1)}, u32[]{:S(2)}) copy-start(bf16[1,1,1,768,128]{4,3,2,1,0:T(8,128)(2,1)} %param.11) | copy-start | bytes 589828
  3.3 0.9 %copy-start.1 = (bf16[1,1,1,768,128]{4,3,2,1,0:T(8,128)(2,1)S(1)}, bf16[1,1,1,768,128]{4,3,2,1,0:T(8,128)(2,1)}, u32[]{:S(2)}) copy-start(bf16[1,1,1,768,128]{4,3,2,1,0:T(8,128)(2,1)} %param.12) | copy-start | bytes 589828
  4.2 0.8 %copy-start.2 = (bf16[128,128]{1,0:T(8,128)(2,1)S(1)}, bf16[128,128]{1,0:T(8,128)(2,1)}, u32[]{:S(2)}) copy-start(bf16[128,128]{1,0:T(8,128)(2,1)} %ref_weight_ref.1) | copy-start | bytes 98308
  5.0 0.7 %copy-start.3 = (s32[1,1,1,768]{3,2,1,0:T(1,128)S(1)}, s32[1,1,1,768]{3,2,1,0:T(1,128)}, u32[]{:S(2)}) copy-start(s32[1,1,1,768]{3,2,1,0:T(1,128)} %param.18) | copy-start | bytes 9220
  5.7 0.7 copy-start.4
  6.3 0.7 copy-start.5
  7.0 0.7 copy-start.6
  7.6 0.7 copy-start.7

commit v3 on v2

--- a/solution.py
+++ b/solution.py
@@ -21,15 +21,28 @@
 
 def step_kernel(
     sizes, cap, rim_count,
-    feat_ref, ref_feat_ref, rim_ref, nbr_ref, lists_ref, counts_ref, match_ref, labels_ref,
-    weight_ref, ref_weight_ref, cls_ref,
+    feat_hbm, ref_feat_hbm, rim_hbm, nbr_hbm, lists_hbm, counts_hbm, match_hbm, labels_hbm,
+    weight_hbm, ref_weight_hbm, cls_hbm,
     activ_ref, fgrad_ref, wsum_ref, rsum_ref,
     table, onehot, gathered, acc, pgrad, terms, rim, rims, outbox, inbox, gbox, gin,
     recv_x, recv_t, recv_y, part_x, part_t, whole,
+    feat_ref, ref_feat_ref, rim_ref, nbr_ref, lists_ref, counts_ref, match_ref, labels_ref,
+    weight_ref, ref_weight_ref, cls_ref, load_sem,
     rim_send, rim_recv, box_send, box_recv, g_send, g_recv, rs_send, rs_recv, ag_send, ag_recv,
 ):
     offsets = weight_ref.shape[0]
     rows, channels = feat_ref.shape
+    loads = [
+        pltpu.make_async_copy(src, dst, load_sem.at[i])
+        for i, (src, dst) in enumerate((
+            (feat_hbm, feat_ref), (rim_hbm, rim_ref), (ref_feat_hbm, ref_feat_ref),
+            (lists_hbm, lists_ref), (counts_hbm, counts_ref), (nbr_hbm, nbr_ref),
+            (weight_hbm, weight_ref), (ref_weight_hbm, ref_weight_ref), (match_hbm, match_ref),
+            (labels_hbm, labels_ref), (cls_hbm, cls_ref),
+        ))
+    ]
+    for load in loads:
+        load.start()
     groups = table.shape[0] // channels
     own_groups = rows // GROUP
     center = offsets // 2
@@ -80,6 +93,8 @@
                 device_id_type=MESH,
             )
 
+    loads[0].wait()
+    loads[1].wait()
     spot = (lax.broadcasted_iota(jnp.int32, (rows, rim_count), 0) == rim_ref[...]).astype(
         jnp.float32
     ).astype(jnp.bfloat16)
@@ -123,12 +138,15 @@
             device_id_type=MESH,
         )
 
+    for load in loads[2:]:
+        load.wait()
+
     @pl.when(t < n_t - 1)
     def _():
         for d in range(bricks):
             for s in range(cap):
-                block = ref_feat_ref[lists_ref[d * cap + s]]
-                outbox[d, s] = jnp.where(s < counts_ref[d], block, jnp.zeros_like(block))
+                block = ref_feat_ref[lists_ref[d, s]]
+                outbox[d, s] = jnp.where(s < counts_ref[0, d], block, jnp.zeros_like(block))
         for k in range(bricks):
             box_copy(k, False).start()
 
@@ -187,7 +205,7 @@
             box_copy(k, True).wait_recv()
 
     for k in range(rows // BLOCK):
-        where = match_ref[k]
+        where = match_ref[0, k]
         live = (where < bricks * cap) & (t > 0)
         safe = jnp.minimum(where, bricks * cap - 1)
         block = inbox[safe // cap, lax.rem(safe, cap)]
@@ -373,6 +391,13 @@
     ag_finish("gx")
     wsum_ref[...] = whole[pl.ds(0, offsets * channels), :]
     rsum_ref[...] = whole[pl.ds(offsets * channels, channels), :]
+
+
+def finish_kernel(activ_ref, fgrad_ref, wsum_ref, rsum_ref, activ_out, fgrad_out, wsum_out, rsum_out):
+    activ_out[...] = activ_ref[...]
+    fgrad_out[...] = fgrad_ref[...]
+    wsum_out[...] = wsum_ref[...].astype(jnp.float32)
+    rsum_out[...] = rsum_ref[...].astype(jnp.float32)
 
 
 def per_device(
@@ -389,7 +414,6 @@
     term_rows = -(-(offsets + 1) * channels // step) * step
     groups = -(-(rows + 9 * rim_count + 1) // GROUP)
     vmem = pl.BlockSpec(memory_space=pltpu.VMEM)
-    smem = pl.BlockSpec(memory_space=pltpu.SMEM)
     recv, part = [], []
     length = term_rows
     for axis in AXES:
@@ -407,7 +431,7 @@
             jax.ShapeDtypeStruct((offsets * channels, channels), jnp.bfloat16),
             jax.ShapeDtypeStruct((channels, channels), jnp.bfloat16),
         ),
-        in_specs=[vmem, vmem, vmem, vmem, smem, smem, smem, vmem, vmem, vmem, vmem],
+        in_specs=[pl.BlockSpec(memory_space=pltpu.HBM)] * 11,
         out_specs=(vmem,) * 4,
         scratch_shapes=[
             pltpu.VMEM((groups * channels, GROUP), jnp.bfloat16),
@@ -424,11 +448,23 @@
             pltpu.VMEM((9, rim_count, channels), jnp.bfloat16),
             *recv,
             *part,
+            pltpu.VMEM((rows, channels), jnp.bfloat16),
+            pltpu.VMEM((rows // BLOCK, BLOCK, channels), jnp.bfloat16),
+            pltpu.VMEM((1, rim_count), jnp.int32),
+            pltpu.VMEM((offsets, rows), jnp.int32),
+            pltpu.SMEM((bricks, cap), jnp.int32),
+            pltpu.SMEM((1, bricks), jnp.int32),
+            pltpu.SMEM((1, rows // BLOCK), jnp.int32),
+            pltpu.VMEM((1, rows), jnp.int32),
+            pltpu.VMEM((offsets, channels, channels), jnp.bfloat16),
+            pltpu.VMEM((channels, channels), jnp.bfloat16),
+            pltpu.VMEM((1, channels), jnp.bfloat16),
+            dma((11,)),
             dma((9,)), dma((9,)), dma((bricks,)), dma((bricks,)), dma((9,)), dma((9,)),
             dma((peers,)), dma((peers,)), dma((peers,)), dma((peers,)),
         ],
         compiler_params=pltpu.CompilerParams(
-            collective_id=0, has_side_effects=True, vmem_limit_bytes=52 * 1024 * 1024
+            collective_id=0, has_side_effects=True, vmem_limit_bytes=60 * 1024 * 1024
         ),
         name="step",
     )(
@@ -436,17 +472,29 @@
         ref_feat.reshape(rows // BLOCK, BLOCK, channels),
         rim_rows.reshape(1, rim_count),
         nbr.reshape(offsets, rows),
-        send_blocks.reshape(bricks * cap),
-        send_count.reshape(bricks),
-        match_slot.reshape(rows // BLOCK),
+        send_blocks.reshape(bricks, cap),
+        send_count.reshape(1, bricks),
+        match_slot.reshape(1, rows // BLOCK),
         labels.reshape(1, rows),
         conv_weight,
         ref_weight,
         cls_weight.reshape(1, channels),
     )
+    activ, fgrad, wsum, rsum = pl.pallas_call(
+        finish_kernel,
+        out_shape=(
+            jax.ShapeDtypeStruct((rows, channels), jnp.bfloat16),
+            jax.ShapeDtypeStruct((rows, channels), jnp.bfloat16),
+            jax.ShapeDtypeStruct((offsets * channels, channels), jnp.float32),
+            jax.ShapeDtypeStruct((channels, channels), jnp.float32),
+        ),
+        in_specs=[vmem] * 4,
+        out_specs=(vmem,) * 4,
+        name="finish",
+    )(activ, fgrad, wsum, rsum)
     whole = (1, 1, 1, rows, channels)
-    weight_grad = wsum.astype(jnp.float32).reshape(offsets, channels, channels)
-    return activ.reshape(whole), fgrad.reshape(whole), weight_grad, rsum.astype(jnp.float32)
+    weight_grad = wsum.reshape(offsets, channels, channels)
+    return activ.reshape(whole), fgrad.reshape(whole), weight_grad, rsum
 
 
 def solution(mesh):

time: 68.1 us -> 62.6 us (0.919)
  local copies, waits for them, and re-layouts: 9 us -> 2.88 us
  Pallas kernels: 56 us -> 58.8 us
  other arithmetic: 2.03 us -> 0 us
    unnamed x20 -> x1, local copies, waits for them, and re-layouts: 8.92 us -> 1.53 us
    pallas_call x0 -> x1, Pallas kernels: none -> 2.73 us  [per_device(): pl.pallas_call(finish_kernel, out_shape=(jax.ShapeDtypeStruct((rows, chan...]
    reshape x1 -> x0, other arithmetic: 1.4 us -> none  [per_device(): weight_grad = wsum.astype(jnp.float32).reshape(offsets, channels, channels)]
    reshape x1, local copies, waits for them, and re-layouts: 0.08 us -> 1.35 us  [per_device(): send_blocks.reshape(bricks, cap)]
where the time goes in v3:
time: 62.6 us; the launch traced here: 62.3 us
  Pallas kernels  58.8 us (94%)
  local copies, waits for them, and re-layouts  2.88 us (5%)
  between operations  0.64 us (1%)
    pallas_call x1, Pallas kernels, per_device(): pl.pallas_call(functools.partial(step_kernel, sizes, cap, rim_count), out...  56.1 us
    pallas_call x1, Pallas kernels, per_device(): pl.pallas_call(finish_kernel, out_shape=(jax.ShapeDtypeStruct((rows, chan...  2.73 us
    unnamed x1, local copies, waits for them, and re-layouts  1.53 us
    reshape x1, local copies, waits for them, and re-layouts, per_device(): send_blocks.reshape(bricks, cap)  1.35 us

profile of v3, /device:TPU:0, one launch (start us, length us, event | category | flops | bytes accessed | tf_op | source)
XLA Modules:
  0.0 62.3 jit_solution(11931990086379844854)
XLA Ops:
  0.6 1.3 %copy.15.lists_hbm = s32[8,2]{1,0:T(8,128)} copy(s32[8,2]{0,1:T(2,128)} %bitcast.18) | data formatting | bytes 128 | tf_op jit(solution)/shard_map/reshape | solution.py:475
  2.0 1.5 %copy.18 = s32[1,1,1,27,768]{4,3,2,1,0:T(8,128)} copy(s32[1,1,1,27,768]{4,2,3,1,0:T(1,128)} %param.14) | data formatting | bytes 165888
  3.5 56.1 %step.1 = (bf16[768,128]{1,0:T(8,128)(2,1)}, bf16[768,128]{1,0:T(8,128)(2,1)}, bf16[3456,128]{1,0:T(8,128)(2,1)}, bf16[128,128]{1,0:T(8,128)(2,1)}) custom-call(bf16[768,128]{1,0:T(8,128)(2,1)} %bitcast.15, bf16[6,128,128]{2,1,0:T(8,128)(2,1)} %bitcast.16, s32[1,48]{1,0:T(1,128)} %bitcast.19, s32[27,768]{1,0:T(8,128)} %bitcast.14, s32[8,2]{1,0:T(8,128)} %copy.15.lists_hbm, ...), custom_call_target="tpu_custom_call" | custom-call | tf_op jit(solution)/shard_map/step/pallas_call | solution.py:426
  59.6 2.7 %finish.1 = (bf16[768,128]{1,0:T(8,128)(2,1)}, bf16[768,128]{1,0:T(8,128)(2,1)}, f32[3456,128]{1,0:T(8,128)}, f32[128,128]{1,0:T(8,128)}) custom-call(bf16[768,128]{1,0:T(8,128)(2,1)} %get-tuple-element.12.activ_ref, bf16[768,128]{1,0:T(8,128)(2,1)} %get-tuple-element.13.fgrad_ref, bf16[3456,128]{1,0:T(8,128)(2,1)} %get-tuple-element.14.wsum_ref, ...), custom_call_target="tpu_custom_call" | custom-call | tf_op jit(solution)/shard_map/finish/pallas_call | solution.py:483
